TPU v7x, 128 devices: a whole 4x4x4 slice. The times are simulated.
128 devices in a mesh: gx: 4 (over z), gy: 16 (over y, x), lev: 2 (over core).
Axes of the slice: x: 4, y: 4, z: 4, core: 2. Of those that a mesh axis runs over, the one named last changes fastest.
Arguments:
- fine_state: float32 [3, 32, 384, 1536], P(None, 'lev', 'gy', 'gx'), may hold values from -6 to 6
- wind_field: float32 [2, 32, 384, 1536], P(None, 'lev', 'gy', 'gx'), may hold values from -4 to 4
- increment: float32 [3, 32, 96, 384], P(None, 'lev', 'gy', 'gx'), may hold values from -6 to 6
- misfit: float32 [3, 32, 96, 384], P(None, 'lev', 'gy', 'gx'), may hold values from -6 to 6
Outputs:
- fine_next: float32 [3, 32, 384, 1536], P(None, 'lev', 'gy', 'gx')
- gradient: float32 [3, 32, 96, 384], P(None, 'lev', 'gy', 'gx')
All inputs are finite; a program needn't handle non-finite values.
Results may differ from a plain program's by a relative error of at most 0.000078.
Values sent between devices are 32-bit elements; how exact they have to be, the bound alone decides.
A program may use at most 64 MiB of HBM per device.

v0:
```python
import jax
import jax.numpy as jnp
from jax import lax
from jax.sharding import PartitionSpec as P

advect = 0.25
vertical_mix = 0.1
damping = 0.3
descent = 0.5


def with_halo(x, sides, width):
    edges = {}
    for axis, dim in sides:
        count, length = (lax.axis_size(axis), x.shape[dim])
        up = [(i, (i + 1) % count) for i in range(count)]
        last = lax.slice_in_dim(x, length - width, length, axis=dim)
        first = lax.slice_in_dim(x, 0, width, axis=dim)
        edges[dim] = (
            lax.ppermute(last, axis, up),
            lax.ppermute(first, axis, [(b, a) for a, b in up]),
        )
    done = []
    for _, dim in sides:
        low, high = edges[dim]
        around = [(width, width) if d in done else (0, 0) for d in range(x.ndim)]
        x = jnp.concatenate([jnp.pad(low, around), x, jnp.pad(high, around)], axis=dim)
        done.append(dim)
    return x


def with_halo_2(block, sides, width):
    for axis, dim in sides:
        count = lax.axis_size(axis)
        forward = [(i, i + 1) for i in range(count - 1)]
        forward.append((count - 1, 0))
        backward = [(target, source) for source, target in forward]
        low = lax.ppermute(
            lax.slice_in_dim(block, block.shape[dim] - width, None, axis=dim), axis, forward
        )
        high = lax.ppermute(lax.slice_in_dim(block, 0, width, axis=dim), axis, backward)
        block = jnp.concatenate([low, block, high], axis=dim)
    return block


def mixing():
    return jnp.array([0.05, 0.1, 0.2], jnp.float32).reshape(3, 1, 1, 1)


def laplace_terms(padded):
    center = padded[:, 1:-1, 1:-1, 1:-1]
    planar = (
        padded[:, 1:-1, 1:-1, 2:]
        + padded[:, 1:-1, 1:-1, :-2]
        + padded[:, 1:-1, 2:, 1:-1]
        + padded[:, 1:-1, :-2, 1:-1]
        - 4.0 * center
    )
    column = padded[:, 2:, 1:-1, 1:-1] + padded[:, :-2, 1:-1, 1:-1] - 2.0 * center
    return (center, mixing() * planar + vertical_mix * column)


def forward_linear(padded, wind_center):
    center, spread = laplace_terms(padded)
    along_x = 0.5 * (padded[:, 1:-1, 1:-1, 2:] - padded[:, 1:-1, 1:-1, :-2])
    along_y = 0.5 * (padded[:, 1:-1, 2:, 1:-1] - padded[:, 1:-1, :-2, 1:-1])
    return center - advect * (wind_center[0] * along_x + wind_center[1] * along_y) + spread


def adjoint_linear(padded, wind_pad):
    center, spread = laplace_terms(padded)
    flux_x = wind_pad[0] * padded
    flux_y = wind_pad[1] * padded
    along_x = 0.5 * (flux_x[:, 1:-1, 1:-1, 2:] - flux_x[:, 1:-1, 1:-1, :-2])
    along_y = 0.5 * (flux_y[:, 1:-1, 2:, 1:-1] - flux_y[:, 1:-1, :-2, 1:-1])
    return center + advect * (along_x + along_y) + spread


def slope(state):
    squashed = jnp.tanh(state)
    return damping * (1.0 - squashed * squashed)


def restrict(values):
    dims_now = values.shape
    blocks = values.reshape(dims_now[0], dims_now[1], dims_now[2] // 4, 4, dims_now[3] // 4, 4)
    return jnp.mean(blocks, axis=(3, 5))


def coarse_chain(extend, cstate, cwinds, increment, misfit):
    variables = cstate.shape[0]
    stacked = extend(jnp.concatenate([cwinds, cstate, increment], axis=0))
    wind_pad = stacked[:2]
    trajectory = forward_linear(stacked[2 : 2 + variables], cwinds) - damping * jnp.tanh(cstate)
    delta_one = forward_linear(stacked[2 + variables :], cwinds) - slope(cstate) * increment
    delta_two = forward_linear(extend(delta_one), cwinds) - slope(trajectory) * delta_one
    residual = delta_two - misfit
    adjoint_one = adjoint_linear(extend(residual), wind_pad) - slope(trajectory) * residual
    adjoint_zero = adjoint_linear(extend(adjoint_one), wind_pad) - slope(cstate) * adjoint_one
    gradient = increment + adjoint_zero
    return (gradient, increment - descent * gradient)


def zero_ends(padded, dimension, position_now, members):
    position = lax.broadcasted_iota(jnp.int32, padded.shape, dimension)
    first = jnp.logical_and(position_now == 0, position == 0)
    final = jnp.logical_and(position_now == members - 1, position == padded.shape[dimension] - 1)
    return jnp.where(jnp.logical_or(first, final), jnp.zeros_like(padded), padded)


def column_table(coarse_cols):
    offset = 0
    fine_cols = 4 * coarse_cols + 2 * offset
    position = lax.broadcasted_iota(jnp.int32, (coarse_cols + 2, fine_cols), 1) - offset
    source = lax.broadcasted_iota(jnp.int32, (coarse_cols + 2, fine_cols), 0)
    scaled = 4 * position + 10
    beneath = scaled // 16
    fraction = (scaled % 16).astype(jnp.float32) / 16.0
    return jnp.where(source == beneath, 1.0 - fraction, 0.0) + jnp.where(
        source == beneath + 1, fraction, 0.0
    )


def prolong_columns(padded):
    table = column_table(padded.shape[3] - 2)
    return jnp.dot(
        padded, table, precision=lax.Precision.HIGHEST, preferred_element_type=jnp.float32
    )


def prolong_rows(padded):
    number = padded.shape[2] - 2
    left = padded[:, :, 0:number]
    middle = padded[:, :, 1 : number + 1]
    right = padded[:, :, 2 : number + 2]
    pieces = [
        0.375 * left + 0.625 * middle,
        0.125 * left + 0.875 * middle,
        0.875 * middle + 0.125 * right,
        0.625 * middle + 0.375 * right,
    ]
    joined = jnp.stack(pieces, axis=3)
    target = list(padded.shape)
    target[2] = 4 * number
    result = joined.reshape(target)
    return result


def per_device(fine_state, wind_field, increment, misfit):
    row_index = lax.axis_index("gy")
    row_count = lax.axis_size("gy")
    level_index = lax.axis_index("lev")
    level_count = lax.axis_size("lev")

    def fix_levels(padded):
        return zero_ends(padded, 1, level_index, level_count)

    def fix_rows(padded):
        return zero_ends(padded, 2, row_index, row_count)

    cstate = restrict(fine_state)
    cwinds = restrict(wind_field)

    def extend(values):
        return fix_rows(fix_levels(with_halo(values, (("gx", 3), ("gy", 2), ("lev", 1)), 1)))

    gradient, updated = coarse_chain(extend, cstate, cwinds, increment, misfit)
    planar_pad = fix_rows(with_halo_2(updated, (("gx", 3), ("gy", 2)), 1))
    coarse_pad = jnp.pad(planar_pad, ((0, 0), (1, 1), (0, 0), (0, 0)))
    fine_new = fine_state + prolong_rows(prolong_columns(coarse_pad[:, 1:-1]))
    new_pad = fix_rows(fix_levels(with_halo_2(fine_new, (("gx", 3), ("gy", 2), ("lev", 1)), 1)))
    fine_next = forward_linear(new_pad, wind_field) - damping * jnp.tanh(fine_new)
    return (fine_next, gradient)


def solution(mesh):
    in_specs = (
        P(None, "lev", "gy", "gx"),
        P(None, "lev", "gy", "gx"),
        P(None, "lev", "gy", "gx"),
        P(None, "lev", "gy", "gx"),
    )
    out_specs = (P(None, "lev", "gy", "gx"), P(None, "lev", "gy", "gx"))
    return jax.shard_map(
        per_device, mesh=mesh, in_specs=in_specs, out_specs=out_specs, check_vma=False
    )
```

profile of v0, /device:TPU:1, one launch (start us, length us, event | category | flops | bytes accessed | tf_op | source)
XLA Modules:
  0.0 134.3 jit_solution(10835341016173942093)
XLA Ops:
  0.6 9.8 %copy.200 = f32[3,16,24,384]{1,3,2,0:T(8,128)} copy(f32[3,16,24,384]{3,2,1,0:T(8,128)} %param.10) | data formatting | bytes 3538944 | tf_op args[0]
  10.4 11.5 %reduce_sum.19 = f32[3,16,6,96]{1,3,2,0:T(8,128)S(1)} reduce(f32[3,16,6,4,96,4]{1,5,4,3,2,0:T(4,128)} %bitcast.30, f32[]{:T(128)} %constant.31.clone.1), dimensions={3,5}, to_apply=%region_1.0 | reduce | flops 414720 | bytes 1880068 | tf_op jit(solution)/shard_map/reduce_sum | solution.py:87
  23.2 5.6 %copy.198 = f32[2,16,24,384]{1,3,2,0:T(8,128)} copy(f32[2,16,24,384]{3,2,1,0:T(8,128)S(1)} %copy-done.2) | data formatting | bytes 2359296 | tf_op args[1]
  28.8 6.9 %reduce_sum.18 = f32[2,16,6,96]{1,3,2,0:T(8,128)S(1)} reduce(f32[2,16,6,4,96,4]{1,5,4,3,2,0:T(4,128)} %bitcast.31, f32[]{:T(128)} %constant.31.clone.1), dimensions={3,5}, to_apply=%region_0.0 | reduce | flops 276480 | bytes 1253380 | tf_op jit(solution)/shard_map/reduce_sum | solution.py:87
  36.1 2.5 %collective-permute-start.2 = (f32[8,16,6,1]{3,1,2,0:T(8,128)S(1)}, f32[8,16,6,1]{3,1,2,0:T(8,128)S(1)}, u32[]{:S(2)}, u32[]{:S(2)}) collective-permute-start(f32[8,16,6,1]{3,1,2,0:T(8,128)S(1)} %get-tuple-element.36), channel_id=1, source_target_pairs={{0,32},{32,64},{64,96},{96,0},{1,33},{33,65},{65,97},{97,1},{2,34}... | collective-permute-start | bytes 9224 | tf_op jit(solution)/shard_map/ppermute | solution.py:20
  38.6 2.2 %collective-permute-start.3 = (f32[8,16,6,1]{3,1,2,0:T(8,128)S(1)}, f32[8,16,6,1]{3,1,2,0:T(8,128)S(1)}, u32[]{:S(2)}, u32[]{:S(2)}) collective-permute-start(f32[8,16,6,1]{3,1,2,0:T(8,128)S(1)} %get-tuple-element.37), channel_id=1, source_target_pairs={{32,0},{64,32},{96,64},{0,96},{33,1},{65,33},{97,65},{1,97},{34,2}... | collective-permute-start | bytes 9224 | tf_op jit(solution)/shard_map/ppermute | solution.py:21
  42.2 3.8 %collective-permute-start.4 = (f32[8,16,1,96]{3,1,2,0:T(8,128)S(1)}, f32[8,16,1,96]{3,1,2,0:T(8,128)S(1)}, u32[]{:S(2)}, u32[]{:S(2)}) collective-permute-start(f32[8,16,1,96]{3,1,2,0:T(8,128)S(1)} %get-tuple-element.41), channel_id=1, source_target_pairs={{2,0},{4,2},{6,4},{8,6},{10,8},{12,10},{14,12},{16,14},{18,16},{20... | collective-permute-start | bytes 147464 | tf_op jit(solution)/shard_map/ppermute | solution.py:21
  51.1 2.3 %collective-permute-start.9 = (f32[3,16,6,1]{3,1,2,0:T(8,128)S(1)}, f32[3,16,6,1]{3,1,2,0:T(8,128)S(1)}, u32[]{:S(2)}, u32[]{:S(2)}) collective-permute-start(f32[3,16,6,1]{3,1,2,0:T(8,128)S(1)} %get-tuple-element.59), channel_id=1, source_target_pairs={{32,0},{64,32},{96,64},{0,96},{33,1},{65,33},{97,65},{1,97},{34,2}... | collective-permute-start | bytes 3464 | tf_op jit(solution)/shard_map/ppermute | solution.py:21
  53.4 4.9 %collective-permute-start.10 = (f32[3,16,1,96]{3,1,2,0:T(8,128)S(1)}, f32[3,16,1,96]{3,1,2,0:T(8,128)S(1)}, u32[]{:S(2)}, u32[]{:S(2)}) collective-permute-start(f32[3,16,1,96]{3,1,2,0:T(8,128)S(1)} %get-tuple-element.63), channel_id=1, source_target_pairs={{2,0},{4,2},{6,4},{8,6},{10,8},{12,10},{14,12},{16,14},{18,16},{20... | collective-permute-start | bytes 55304 | tf_op jit(solution)/shard_map/ppermute | solution.py:21
  58.3 2.1 %collective-permute-start.11 = (f32[3,1,6,96]{3,1,2,0:T(1,128)S(1)}, f32[3,1,6,96]{3,1,2,0:T(1,128)S(1)}, u32[]{:S(2)}, u32[]{:S(2)}) collective-permute-start(f32[3,1,6,96]{3,1,2,0:T(1,128)S(1)} %get-tuple-element.61), channel_id=1, source_target_pairs={{1,0},{0,1},{3,2},{2,3},{5,4},{4,5},{7,6},{6,7},{9,8},{8,9},{11,10... | collective-permute-start | bytes 20744 | tf_op jit(solution)/shard_map/ppermute | solution.py:21
  61.6 2.7 %collective-permute-done.7 = f32[3,16,1,96]{3,1,2,0:T(8,128)S(1)} collective-permute-done((f32[3,16,1,96]{3,1,2,0:T(8,128)S(1)}, f32[3,16,1,96]{3,1,2,0:T(8,128)S(1)}, u32[]{:S(2)}, u32[]{:S(2)}) %collective-permute-start.7) | collective-permute-done | bytes 18464 | tf_op jit(solution)/shard_map/ppermute | solution.py:20
  65.3 2.7 %collective-permute-start.15 = (f32[3,16,6,1]{3,1,2,0:T(8,128)S(1)}, f32[3,16,6,1]{3,1,2,0:T(8,128)S(1)}, u32[]{:S(2)}, u32[]{:S(2)}) collective-permute-start(f32[3,16,6,1]{3,1,2,0:T(8,128)S(1)} %get-tuple-element.57), channel_id=1, source_target_pairs={{32,0},{64,32},{96,64},{0,96},{33,1},{65,33},{97,65},{1,97},{34,2}... | collective-permute-start | bytes 3464 | tf_op jit(solution)/shard_map/ppermute | solution.py:21
  68.0 4.8 %collective-permute-start.16 = (f32[3,16,1,96]{3,1,2,0:T(8,128)S(1)}, f32[3,16,1,96]{3,1,2,0:T(8,128)S(1)}, u32[]{:S(2)}, u32[]{:S(2)}) collective-permute-start(f32[3,16,1,96]{3,1,2,0:T(8,128)S(1)} %get-tuple-element.55), channel_id=1, source_target_pairs={{2,0},{4,2},{6,4},{8,6},{10,8},{12,10},{14,12},{16,14},{18,16},{20... | collective-permute-start | bytes 55304 | tf_op jit(solution)/shard_map/ppermute | solution.py:21
  72.8 4.4 %collective-permute-start.12 = (f32[3,1,6,96]{3,1,2,0:T(1,128)S(1)}, f32[3,1,6,96]{3,1,2,0:T(1,128)S(1)}, u32[]{:S(2)}, u32[]{:S(2)}) collective-permute-start(f32[3,1,6,96]{3,1,2,0:T(1,128)S(1)} %get-tuple-element.52), channel_id=1, source_target_pairs={{0,1},{1,0},{2,3},{3,2},{4,5},{5,4},{6,7},{7,6},{8,9},{9,8},{10,11... | collective-permute-start | bytes 20744 | tf_op jit(solution)/shard_map/ppermute | solution.py:20
  79.3 2.7 %collective-permute-start.21 = (f32[3,16,6,1]{3,1,2,0:T(8,128)S(1)}, f32[3,16,6,1]{3,1,2,0:T(8,128)S(1)}, u32[]{:S(2)}, u32[]{:S(2)}) collective-permute-start(f32[3,16,6,1]{3,1,2,0:T(8,128)S(1)} %get-tuple-element.51), channel_id=1, source_target_pairs={{32,0},{64,32},{96,64},{0,96},{33,1},{65,33},{97,65},{1,97},{34,2}... | collective-permute-start | bytes 3464 | tf_op jit(solution)/shard_map/ppermute | solution.py:21
  81.9 4.8 %collective-permute-start.22 = (f32[3,16,1,96]{3,1,2,0:T(8,128)S(1)}, f32[3,16,1,96]{3,1,2,0:T(8,128)S(1)}, u32[]{:S(2)}, u32[]{:S(2)}) collective-permute-start(f32[3,16,1,96]{3,1,2,0:T(8,128)S(1)} %get-tuple-element.49), channel_id=1, source_target_pairs={{2,0},{4,2},{6,4},{8,6},{10,8},{12,10},{14,12},{16,14},{18,16},{20... | collective-permute-start | bytes 55304 | tf_op jit(solution)/shard_map/ppermute | solution.py:21
  91.2 2.7 %collective-permute-start.25 = (f32[3,16,6,1]{3,1,2,0:T(8,128)S(1)}, f32[3,16,6,1]{3,1,2,0:T(8,128)S(1)}, u32[]{:S(2)}, u32[]{:S(2)}) collective-permute-start(f32[3,16,6,1]{3,1,2,0:T(8,128)S(1)} %get-tuple-element.45), channel_id=1, source_target_pairs={{32,0},{64,32},{96,64},{0,96},{33,1},{65,33},{97,65},{1,97},{34,2}... | collective-permute-start | bytes 3464 | tf_op jit(solution)/shard_map/ppermute | solution.py:41
  93.9 3.3 %collective-permute-done.24 = f32[3,16,6,1]{3,1,2,0:T(8,128)S(1)} collective-permute-done((f32[3,16,6,1]{3,1,2,0:T(8,128)S(1)}, f32[3,16,6,1]{3,1,2,0:T(8,128)S(1)}, u32[]{:S(2)}, u32[]{:S(2)}) %collective-permute-start.24) | collective-permute-done | bytes 1184 | tf_op jit(solution)/shard_map/ppermute | solution.py:38
  97.4 4.8 %collective-permute-start.27 = (f32[3,16,1,98]{3,1,2,0:T(8,128)S(1)}, f32[3,16,1,98]{3,1,2,0:T(8,128)S(1)}, u32[]{:S(2)}, u32[]{:S(2)}) collective-permute-start(f32[3,16,1,98]{3,1,2,0:T(8,128)S(1)} %get-tuple-element.43), channel_id=1, source_target_pairs={{2,0},{4,2},{6,4},{8,6},{10,8},{12,10},{14,12},{16,14},{18,16},{20... | collective-permute-start | bytes 56456 | tf_op jit(solution)/shard_map/ppermute | solution.py:41
  107.4 2.7 %collective-permute-start.29 = (f32[3,16,24,1]{2,1,3,0:T(8,128)S(1)}, f32[3,16,24,1]{2,1,3,0:T(8,128)S(1)}, u32[]{:S(2)}, u32[]{:S(2)}) collective-permute-start(f32[3,16,24,1]{2,1,3,0:T(8,128)S(1)} %copy.213), channel_id=1, source_target_pairs={{32,0},{64,32},{96,64},{0,96},{33,1},{65,33},{97,65},{1,97},{34,2}... | collective-permute-start | bytes 13832 | tf_op jit(solution)/shard_map/ppermute | solution.py:41
  112.1 4.9 %collective-permute-start.31 = (f32[3,16,1,386]{3,1,2,0:T(8,128)S(1)}, f32[3,16,1,386]{3,1,2,0:T(8,128)S(1)}, u32[]{:S(2)}, u32[]{:S(2)}) collective-permute-start(f32[3,16,1,386]{3,1,2,0:T(8,128)S(1)} %get-tuple-element.25), channel_id=1, source_target_pairs={{2,0},{4,2},{6,4},{8,6},{10,8},{12,10},{14,12},{16,14},{18,16},{20... | collective-permute-start | bytes 222344 | tf_op jit(solution)/shard_map/ppermute | solution.py:41
  119.7 5.0 %collective-permute-start.32 = (f32[3,1,26,386]{3,1,2,0:T(1,128)S(1)}, f32[3,1,26,386]{3,1,2,0:T(1,128)S(1)}, u32[]{:S(2)}, u32[]{:S(2)}) collective-permute-start(f32[3,1,26,386]{3,1,2,0:T(1,128)S(1)} %get-tuple-element.22), channel_id=1, source_target_pairs={{0,1},{1,0},{2,3},{3,2},{4,5},{5,4},{6,7},{7,6},{8,9},{9,8},{10,11... | collective-permute-start | bytes 361304 | tf_op jit(solution)/shard_map/ppermute | solution.py:38
  126.1 3.3 %fusion = f32[3,18,26,386]{3,1,2,0:T(8,128)S(1)} fusion(f32[3,1,26,386]{3,1,2,0:T(1,128)S(1)} %collective-permute-done.33, f32[3,16,1,386]{3,1,2,0:T(8,128)S(1)} %collective-permute-done.31, f32[3,16,24,1]{3,1,2,0:T(8,128)S(1)} %copy.215, f32[3,16,24,384]{3,1,2,0:T(8,128)S(1)} %copy_add_fusion, f32[3,16,24,1]{3,1,2,0:T(8,128)S(1)} %copy.214, ...), kind=kLoop, calls=%fused_computation.1 | loop fusion | flops 4335552 | bytes 4335596 | tf_op jit(solution)/shard_map/jit(_where)/select_n | solution.py:108
  129.4 3.2 %fusion.5 = f32[3,16,24,384]{3,1,2,0:T(8,128)S(1)} fusion(f32[3,18,26,386]{3,1,2,0:T(8,128)S(1)} %fusion, f32[3,16,24,384]{3,1,2,0:T(8,128)S(1)} %copy_add_fusion, f32[3]{0:T(128)S(1)} %copy-done.5, f32[16,24,384]{2,0,1:T(8,128)S(1)} %copy.217, f32[16,24,384]{2,0,1:T(8,128)S(1)} %copy.216), kind=kLoop, calls=%fused_computation.7 | loop fusion | flops 9289728 | bytes 17104908 | tf_op jit(solution)/shard_map/sub | solution.py:172
  (123 shorter events, 29.9 us)
Async XLA Ops:
  36.1 13.5 %collective-permute-start.2 = (f32[8,16,6,1]{3,1,2,0:T(8,128)S(1)}, f32[8,16,6,1]{3,1,2,0:T(8,128)S(1)}, u32[]{:S(2)}, u32[]{:S(2)}) collective-permute-start(f32[8,16,6,1]{3,1,2,0:T(8,128)S(1)} %get-tuple-element.36), channel_id=1, source_target_pairs={{0,32},{32,64},{64,96},{96,0},{1,33},{33,65},{65,97},{97,1},{2,34}... | collective-permute-start | bytes 9224 | tf_op jit(solution)/shard_map/ppermute | solution.py:20
  38.6 10.9 %collective-permute-start.3 = (f32[8,16,6,1]{3,1,2,0:T(8,128)S(1)}, f32[8,16,6,1]{3,1,2,0:T(8,128)S(1)}, u32[]{:S(2)}, u32[]{:S(2)}) collective-permute-start(f32[8,16,6,1]{3,1,2,0:T(8,128)S(1)} %get-tuple-element.37), channel_id=1, source_target_pairs={{32,0},{64,32},{96,64},{0,96},{33,1},{65,33},{97,65},{1,97},{34,2}... | collective-permute-start | bytes 9224 | tf_op jit(solution)/shard_map/ppermute | solution.py:21
  40.9 8.7 %collective-permute-start.1 = (f32[8,16,1,96]{3,1,2,0:T(8,128)S(1)}, f32[8,16,1,96]{3,1,2,0:T(8,128)S(1)}, u32[]{:S(2)}, u32[]{:S(2)}) collective-permute-start(f32[8,16,1,96]{3,1,2,0:T(8,128)S(1)} %get-tuple-element.40), channel_id=1, source_target_pairs={{0,2},{2,4},{4,6},{6,8},{8,10},{10,12},{12,14},{14,16},{16,18},{18... | collective-permute-start | bytes 147464 | tf_op jit(solution)/shard_map/ppermute | solution.py:20
  42.2 7.4 %collective-permute-start.4 = (f32[8,16,1,96]{3,1,2,0:T(8,128)S(1)}, f32[8,16,1,96]{3,1,2,0:T(8,128)S(1)}, u32[]{:S(2)}, u32[]{:S(2)}) collective-permute-start(f32[8,16,1,96]{3,1,2,0:T(8,128)S(1)} %get-tuple-element.41), channel_id=1, source_target_pairs={{2,0},{4,2},{6,4},{8,6},{10,8},{12,10},{14,12},{16,14},{18,16},{20... | collective-permute-start | bytes 147464 | tf_op jit(solution)/shard_map/ppermute | solution.py:21
  50.6 9.8 %collective-permute-start.8 = (f32[3,16,6,1]{3,1,2,0:T(8,128)S(1)}, f32[3,16,6,1]{3,1,2,0:T(8,128)S(1)}, u32[]{:S(2)}, u32[]{:S(2)}) collective-permute-start(f32[3,16,6,1]{3,1,2,0:T(8,128)S(1)} %get-tuple-element.58), channel_id=1, source_target_pairs={{0,32},{32,64},{64,96},{96,0},{1,33},{33,65},{65,97},{97,1},{2,34}... | collective-permute-start | bytes 3464 | tf_op jit(solution)/shard_map/ppermute | solution.py:20
  51.1 9.6 %collective-permute-start.9 = (f32[3,16,6,1]{3,1,2,0:T(8,128)S(1)}, f32[3,16,6,1]{3,1,2,0:T(8,128)S(1)}, u32[]{:S(2)}, u32[]{:S(2)}) collective-permute-start(f32[3,16,6,1]{3,1,2,0:T(8,128)S(1)} %get-tuple-element.59), channel_id=1, source_target_pairs={{32,0},{64,32},{96,64},{0,96},{33,1},{65,33},{97,65},{1,97},{34,2}... | collective-permute-start | bytes 3464 | tf_op jit(solution)/shard_map/ppermute | solution.py:21
  53.4 8.2 %collective-permute-start.10 = (f32[3,16,1,96]{3,1,2,0:T(8,128)S(1)}, f32[3,16,1,96]{3,1,2,0:T(8,128)S(1)}, u32[]{:S(2)}, u32[]{:S(2)}) collective-permute-start(f32[3,16,1,96]{3,1,2,0:T(8,128)S(1)} %get-tuple-element.63), channel_id=1, source_target_pairs={{2,0},{4,2},{6,4},{8,6},{10,8},{12,10},{14,12},{16,14},{18,16},{20... | collective-permute-start | bytes 55304 | tf_op jit(solution)/shard_map/ppermute | solution.py:21
  58.3 6.0 %collective-permute-start.7 = (f32[3,16,1,96]{3,1,2,0:T(8,128)S(1)}, f32[3,16,1,96]{3,1,2,0:T(8,128)S(1)}, u32[]{:S(2)}, u32[]{:S(2)}) collective-permute-start(f32[3,16,1,96]{3,1,2,0:T(8,128)S(1)} %get-tuple-element.62), channel_id=1, source_target_pairs={{0,2},{2,4},{4,6},{6,8},{8,10},{10,12},{12,14},{14,16},{16,18},{18... | collective-permute-start | bytes 55304 | tf_op jit(solution)/shard_map/ppermute | solution.py:20
  65.2 11.9 %collective-permute-start.14 = (f32[3,16,6,1]{3,1,2,0:T(8,128)S(1)}, f32[3,16,6,1]{3,1,2,0:T(8,128)S(1)}, u32[]{:S(2)}, u32[]{:S(2)}) collective-permute-start(f32[3,16,6,1]{3,1,2,0:T(8,128)S(1)} %get-tuple-element.56), channel_id=1, source_target_pairs={{0,32},{32,64},{64,96},{96,0},{1,33},{33,65},{65,97},{97,1},{2,34}... | collective-permute-start | bytes 3464 | tf_op jit(solution)/shard_map/ppermute | solution.py:20
  65.3 11.8 %collective-permute-start.15 = (f32[3,16,6,1]{3,1,2,0:T(8,128)S(1)}, f32[3,16,6,1]{3,1,2,0:T(8,128)S(1)}, u32[]{:S(2)}, u32[]{:S(2)}) collective-permute-start(f32[3,16,6,1]{3,1,2,0:T(8,128)S(1)} %get-tuple-element.57), channel_id=1, source_target_pairs={{32,0},{64,32},{96,64},{0,96},{33,1},{65,33},{97,65},{1,97},{34,2}... | collective-permute-start | bytes 3464 | tf_op jit(solution)/shard_map/ppermute | solution.py:21
  68.0 10.3 %collective-permute-start.13 = (f32[3,16,1,96]{3,1,2,0:T(8,128)S(1)}, f32[3,16,1,96]{3,1,2,0:T(8,128)S(1)}, u32[]{:S(2)}, u32[]{:S(2)}) collective-permute-start(f32[3,16,1,96]{3,1,2,0:T(8,128)S(1)} %get-tuple-element.54), channel_id=1, source_target_pairs={{0,2},{2,4},{4,6},{6,8},{8,10},{10,12},{12,14},{14,16},{16,18},{18... | collective-permute-start | bytes 55304 | tf_op jit(solution)/shard_map/ppermute | solution.py:20
  68.0 10.3 %collective-permute-start.16 = (f32[3,16,1,96]{3,1,2,0:T(8,128)S(1)}, f32[3,16,1,96]{3,1,2,0:T(8,128)S(1)}, u32[]{:S(2)}, u32[]{:S(2)}) collective-permute-start(f32[3,16,1,96]{3,1,2,0:T(8,128)S(1)} %get-tuple-element.55), channel_id=1, source_target_pairs={{2,0},{4,2},{6,4},{8,6},{10,8},{12,10},{14,12},{16,14},{18,16},{20... | collective-permute-start | bytes 55304 | tf_op jit(solution)/shard_map/ppermute | solution.py:21
  72.8 5.2 %collective-permute-start.12 = (f32[3,1,6,96]{3,1,2,0:T(1,128)S(1)}, f32[3,1,6,96]{3,1,2,0:T(1,128)S(1)}, u32[]{:S(2)}, u32[]{:S(2)}) collective-permute-start(f32[3,1,6,96]{3,1,2,0:T(1,128)S(1)} %get-tuple-element.52), channel_id=1, source_target_pairs={{0,1},{1,0},{2,3},{3,2},{4,5},{5,4},{6,7},{7,6},{8,9},{9,8},{10,11... | collective-permute-start | bytes 20744 | tf_op jit(solution)/shard_map/ppermute | solution.py:20
  79.2 9.3 %collective-permute-start.20 = (f32[3,16,6,1]{3,1,2,0:T(8,128)S(1)}, f32[3,16,6,1]{3,1,2,0:T(8,128)S(1)}, u32[]{:S(2)}, u32[]{:S(2)}) collective-permute-start(f32[3,16,6,1]{3,1,2,0:T(8,128)S(1)} %get-tuple-element.50), channel_id=1, source_target_pairs={{0,32},{32,64},{64,96},{96,0},{1,33},{33,65},{65,97},{97,1},{2,34}... | collective-permute-start | bytes 3464 | tf_op jit(solution)/shard_map/ppermute | solution.py:20
  79.3 9.2 %collective-permute-start.21 = (f32[3,16,6,1]{3,1,2,0:T(8,128)S(1)}, f32[3,16,6,1]{3,1,2,0:T(8,128)S(1)}, u32[]{:S(2)}, u32[]{:S(2)}) collective-permute-start(f32[3,16,6,1]{3,1,2,0:T(8,128)S(1)} %get-tuple-element.51), channel_id=1, source_target_pairs={{32,0},{64,32},{96,64},{0,96},{33,1},{65,33},{97,65},{1,97},{34,2}... | collective-permute-start | bytes 3464 | tf_op jit(solution)/shard_map/ppermute | solution.py:21
  81.9 7.7 %collective-permute-start.19 = (f32[3,16,1,96]{3,1,2,0:T(8,128)S(1)}, f32[3,16,1,96]{3,1,2,0:T(8,128)S(1)}, u32[]{:S(2)}, u32[]{:S(2)}) collective-permute-start(f32[3,16,1,96]{3,1,2,0:T(8,128)S(1)} %get-tuple-element.48), channel_id=1, source_target_pairs={{0,2},{2,4},{4,6},{6,8},{8,10},{10,12},{12,14},{14,16},{16,18},{18... | collective-permute-start | bytes 55304 | tf_op jit(solution)/shard_map/ppermute | solution.py:20
  81.9 7.7 %collective-permute-start.22 = (f32[3,16,1,96]{3,1,2,0:T(8,128)S(1)}, f32[3,16,1,96]{3,1,2,0:T(8,128)S(1)}, u32[]{:S(2)}, u32[]{:S(2)}) collective-permute-start(f32[3,16,1,96]{3,1,2,0:T(8,128)S(1)} %get-tuple-element.49), channel_id=1, source_target_pairs={{2,0},{4,2},{6,4},{8,6},{10,8},{12,10},{14,12},{16,14},{18,16},{20... | collective-permute-start | bytes 55304 | tf_op jit(solution)/shard_map/ppermute | solution.py:21
  91.1 6.1 %collective-permute-start.24 = (f32[3,16,6,1]{3,1,2,0:T(8,128)S(1)}, f32[3,16,6,1]{3,1,2,0:T(8,128)S(1)}, u32[]{:S(2)}, u32[]{:S(2)}) collective-permute-start(f32[3,16,6,1]{3,1,2,0:T(8,128)S(1)} %get-tuple-element.44), channel_id=1, source_target_pairs={{0,32},{32,64},{64,96},{96,0},{1,33},{33,65},{65,97},{97,1},{2,34}... | collective-permute-start | bytes 3464 | tf_op jit(solution)/shard_map/ppermute | solution.py:38
  91.2 6.0 %collective-permute-start.25 = (f32[3,16,6,1]{3,1,2,0:T(8,128)S(1)}, f32[3,16,6,1]{3,1,2,0:T(8,128)S(1)}, u32[]{:S(2)}, u32[]{:S(2)}) collective-permute-start(f32[3,16,6,1]{3,1,2,0:T(8,128)S(1)} %get-tuple-element.45), channel_id=1, source_target_pairs={{32,0},{64,32},{96,64},{0,96},{33,1},{65,33},{97,65},{1,97},{34,2}... | collective-permute-start | bytes 3464 | tf_op jit(solution)/shard_map/ppermute | solution.py:41
  97.4 6.1 %collective-permute-start.26 = (f32[3,16,1,98]{3,1,2,0:T(8,128)S(1)}, f32[3,16,1,98]{3,1,2,0:T(8,128)S(1)}, u32[]{:S(2)}, u32[]{:S(2)}) collective-permute-start(f32[3,16,1,98]{3,1,2,0:T(8,128)S(1)} %get-tuple-element.42), channel_id=1, source_target_pairs={{0,2},{2,4},{4,6},{6,8},{8,10},{10,12},{12,14},{14,16},{16,18},{18... | collective-permute-start | bytes 56456 | tf_op jit(solution)/shard_map/ppermute | solution.py:38
  97.4 6.0 %collective-permute-start.27 = (f32[3,16,1,98]{3,1,2,0:T(8,128)S(1)}, f32[3,16,1,98]{3,1,2,0:T(8,128)S(1)}, u32[]{:S(2)}, u32[]{:S(2)}) collective-permute-start(f32[3,16,1,98]{3,1,2,0:T(8,128)S(1)} %get-tuple-element.43), channel_id=1, source_target_pairs={{2,0},{4,2},{6,4},{8,6},{10,8},{12,10},{14,12},{16,14},{18,16},{20... | collective-permute-start | bytes 56456 | tf_op jit(solution)/shard_map/ppermute | solution.py:41
  111.8 7.1 %collective-permute-start.30 = (f32[3,16,1,386]{3,1,2,0:T(8,128)S(1)}, f32[3,16,1,386]{3,1,2,0:T(8,128)S(1)}, u32[]{:S(2)}, u32[]{:S(2)}) collective-permute-start(f32[3,16,1,386]{3,1,2,0:T(8,128)S(1)} %get-tuple-element.24), channel_id=1, source_target_pairs={{0,2},{2,4},{4,6},{6,8},{8,10},{10,12},{12,14},{14,16},{16,18},{18... | collective-permute-start | bytes 222344 | tf_op jit(solution)/shard_map/ppermute | solution.py:38
  112.1 6.8 %collective-permute-start.31 = (f32[3,16,1,386]{3,1,2,0:T(8,128)S(1)}, f32[3,16,1,386]{3,1,2,0:T(8,128)S(1)}, u32[]{:S(2)}, u32[]{:S(2)}) collective-permute-start(f32[3,16,1,386]{3,1,2,0:T(8,128)S(1)} %get-tuple-element.25), channel_id=1, source_target_pairs={{2,0},{4,2},{6,4},{8,6},{10,8},{12,10},{14,12},{16,14},{18,16},{20... | collective-permute-start | bytes 222344 | tf_op jit(solution)/shard_map/ppermute | solution.py:41
  119.7 6.0 %collective-permute-start.32 = (f32[3,1,26,386]{3,1,2,0:T(1,128)S(1)}, f32[3,1,26,386]{3,1,2,0:T(1,128)S(1)}, u32[]{:S(2)}, u32[]{:S(2)}) collective-permute-start(f32[3,1,26,386]{3,1,2,0:T(1,128)S(1)} %get-tuple-element.22), channel_id=1, source_target_pairs={{0,1},{1,0},{2,3},{3,2},{4,5},{5,4},{6,7},{7,6},{8,9},{9,8},{10,11... | collective-permute-start | bytes 361304 | tf_op jit(solution)/shard_map/ppermute | solution.py:38
  (16 other events, 70.4 us)
where the time goes:
time: 135 us; the launch traced here: 134 us
  starting transfers between devices  63.3 us (47%)
  other arithmetic  30.7 us (23%)
  local copies, waits for them, and re-layouts  22.7 us (17%)
  waiting for transfers between devices  15.8 us (12%)
    ppermute x12, starting transfers between devices, with_halo(): lax.ppermute(first, axis, [(b, a) for a, b in up])  30.5 us
    unnamed x15, local copies, waits for them, and re-layouts  19.4 us
    reduce_sum x2, other arithmetic, restrict(): return jnp.mean(blocks, axis=(3, 5))  18.4 us
    ppermute x5, starting transfers between devices, with_halo_2(): lax.ppermute(lax.slice_in_dim(block, 0, width, axis=dim), axis, backward)  15.1 us
    ppermute x12, starting transfers between devices, with_halo(): lax.ppermute(last, axis, up)  12.2 us
    ppermute x5, waiting for transfers between devices, with_halo_2(): lax.ppermute(lax.slice_in_dim(block, block.shape[dim] - width, None, axis...  7.76 us
    ppermute x12, waiting for transfers between devices, with_halo(): lax.ppermute(last, axis, up)  5.6 us
    ppermute x5, starting transfers between devices, with_halo_2(): lax.ppermute(lax.slice_in_dim(block, block.shape[dim] - width, None, axis...  5.49 us
  transfers between devices with their start and end apart: 34, of which 16 were waited for; matrix products, arithmetic and copies ran while one was open for 1% of the time, Pallas kernels for 0%

commit v1 on v0

v1 whole, which is shorter than its diff:
```python
import functools

import jax
import jax.numpy as jnp
from jax import lax
from jax.experimental import pallas as pl
from jax.experimental.pallas import tpu as pltpu
from jax.sharding import PartitionSpec as P

MESH = pl.DeviceIdType.MESH
F32 = jnp.float32
BF16 = jnp.bfloat16
ANY = pl.BlockSpec(memory_space=pl.ANY)

MIX = (0.05, 0.1, 0.2)
VARS, LEVS, ROWS, COLS = 3, 16, 6, 96
FROWS, FCOLS = 24, 384
NGX, NGY = 4, 16

DEPTH = (4, 4, 4, 4, 4, 5, 5, 5, 3, 3, 3)
FIELDS = len(DEPTH)


def segments_row():
    place, at = {}, 0
    for f in range(FIELDS):
        place[f] = (at, DEPTH[f])
        at += DEPTH[f]
    return place


def segments_corner():
    place, at = {}, 0
    for f in range(FIELDS):
        for k in range(1, DEPTH[f] + 1):
            place[f, k] = (at, DEPTH[f] + 1 - k)
            at += DEPTH[f] + 1 - k
    return place


SEG_ROW = segments_row()
SEG_CORNER = segments_corner()


def split_dot(x, table):
    high = x.astype(BF16)
    low = (x - high.astype(F32)).astype(BF16)
    return jnp.dot(high, table, preferred_element_type=F32) + jnp.dot(
        low, table, preferred_element_type=F32
    )


def exchange_kernel(
    fine, wind, inc, mis,
    e_cw, e_im, xm, fy, fx, fl,
    fs, im_v, half, cu, xs, fys, fxs, table, load_sem, local_sem, send_sem, recv_sem,
):
    gx, gy, lev = lax.axis_index("gx"), lax.axis_index("gy"), lax.axis_index("lev")
    gxs = (lax.rem(gx + 1, NGX), lax.rem(gx + NGX - 1, NGX))
    gys = (lax.rem(gy + 1, NGY), lax.rem(gy + NGY - 1, NGY))
    partner = (gx, gy, 1 - lev)
    near = [(gx, gys[0], lev), (gx, gys[1], lev), (gxs[0], gy, lev), (gxs[1], gy, lev)]
    near += [(gxs[h], gys[s], lev) for h in range(2) for s in range(2)] + [partner]

    barrier = pltpu.get_barrier_semaphore()
    for device in near:
        pl.semaphore_signal(barrier, inc=1, device_id=device, device_id_type=MESH)

    loads = []
    for f in range(VARS):
        loads.append(pltpu.make_async_copy(fine.at[f], fs.at[f], load_sem.at[f]))
    for f in range(2):
        loads.append(pltpu.make_async_copy(wind.at[f], fs.at[3 + f], load_sem.at[3 + f]))
    loads.append(pltpu.make_async_copy(inc, im_v.at[0:3], load_sem.at[5]))
    loads.append(pltpu.make_async_copy(mis, im_v.at[3:6], load_sem.at[6]))
    for copy in loads:
        copy.start()

    source = lax.broadcasted_iota(jnp.int32, (FCOLS, 128), 0) // 4
    target = lax.broadcasted_iota(jnp.int32, (FCOLS, 128), 1)
    table[...] = jnp.where(source == target, 0.0625, 0.0).astype(BF16)

    pl.semaphore_wait(barrier, len(near))

    started = []

    def send(src, dst, device):
        i = len(started)
        copy = pltpu.make_async_remote_copy(
            src_ref=src, dst_ref=dst, send_sem=send_sem.at[i], recv_sem=recv_sem.at[i],
            device_id=device, device_id_type=MESH,
        )
        copy.start()
        started.append(copy)
        return copy

    low_high = lambda d, s: (slice(ROWS - d, ROWS) if s == 0 else slice(0, d))
    lands = lambda d, s: (slice(5 - d, 5) if s == 0 else slice(11, 11 + d))
    tile = pl.ds(pl.multiple_of((1 - lev) * 8, 8), 8)

    y_inc = [
        send(inc.at[:, low_high(5, s)], e_im.at[0:3, lands(5, s), 0:16, :], near[s])
        for s in range(2)
    ]
    y_mis = [
        send(mis.at[:, low_high(3, s)], e_im.at[3:6, lands(3, s), 0:16, :], near[s])
        for s in range(2)
    ]
    own = [
        send(inc.at[:, :, tile, :], e_im.at[0:3, 5:11, 16:24, :], partner),
        send(mis.at[:, :, tile, :], e_im.at[3:6, 5:11, 16:24, :], partner),
    ]

    def coarsen(f):
        loads[f].wait()
        block = fs[f].reshape(LEVS * FROWS, FCOLS)
        half[...] = split_dot(block, table[...])
        for j in range(ROWS):
            total = half[pl.ds(4 * j, LEVS, stride=FROWS), :]
            for a in range(1, 4):
                total += half[pl.ds(4 * j + a, LEVS, stride=FROWS), :]
            cu[f, j] = total

    for f in range(5):
        coarsen(f)
    y_cw = [
        send(cu.at[:, low_high(4, s)], e_cw.at[:, lands(4, s), 0:16, :], near[s])
        for s in range(2)
    ]
    local = pltpu.make_async_copy(cu, e_cw.at[:, 5:11, 0:16, :], local_sem)
    local.start()
    own.append(send(cu.at[:, :, tile, :], e_cw.at[:, 5:11, 16:24, :], partner))
    edge = 15 * (1 - lev)
    own.append(send(fs.at[0:3, edge], fl, partner))

    loads[5].wait()
    loads[6].wait()
    lane = lax.broadcasted_iota(jnp.int32, (LEVS, 128), 1)

    def unit(f, j):
        if f < 5:
            return cu[f, j]
        return jnp.concatenate([im_v[f - 5, j], jnp.zeros((LEVS, 128 - COLS), F32)], axis=1)

    def packed(out, value, h, at, width):
        first = COLS - width if h == 0 else 0
        moved = pltpu.roll(value, (at - first) % 128, 1)
        return jnp.where(jnp.logical_and(lane >= at, lane < at + width), moved, out)

    zero = jnp.zeros((LEVS, 128), F32)
    for h in range(2):
        for s in range(2):
            out = zero
            for (f, k), (at, width) in SEG_CORNER.items():
                out = packed(out, unit(f, ROWS - k if s == 0 else k - 1), h, at, width)
            xs[h, 6 + s] = out
        for j in range(ROWS):
            out = zero
            for f, (at, width) in SEG_ROW.items():
                out = packed(out, unit(f, j), h, at, width)
            xs[h, j] = out
    corner = [
        [
            send(xs.at[h, 6 + s], xm.at[h, 6 + s, 0:16, :], (gxs[h], gys[s], lev))
            for s in range(2)
        ]
        for h in range(2)
    ]
    x_row = [send(xs.at[h, 0:6], xm.at[h, 0:6, 0:16, :], near[2 + h]) for h in range(2)]

    for v in range(VARS):
        for l in range(LEVS):
            fys[0, v, l : l + 1, :] = fs[v, l, FROWS - 1 : FROWS, :]
            fys[1, v, l : l + 1, :] = fs[v, l, 0:1, :]
    y_fine = [send(fys.at[s], fy.at[s], near[s]) for s in range(2)]
    lane8 = lax.broadcasted_iota(jnp.int32, (8, 128), 1)
    for v in range(VARS):
        outs = [jnp.zeros((8, 128), F32)] * 2
        for l in range(LEVS):
            for t in range(3):
                n = 3 * l + t
                first = pltpu.roll(fs[v, l, 8 * t : 8 * t + 8, 0:128], n, 1)
                last = pltpu.roll(fs[v, l, 8 * t : 8 * t + 8, 256:384], (n + 1) % 128, 1)
                outs[0] = jnp.where(lane8 == n, last, outs[0])
                outs[1] = jnp.where(lane8 == n, first, outs[1])
        fxs[0, v] = outs[0]
        fxs[1, v] = outs[1]
    x_fine = [send(fxs.at[h], fx.at[h], near[2 + h]) for h in range(2)]

    relays = []
    for s in range(2):
        y_inc[s].wait_recv()
        rows = lands(5, s)
        relays.append(
            send(e_im.at[0:3, rows, tile, :], e_im.at[0:3, rows, 16:24, :], partner)
        )
    for s in range(2):
        y_mis[s].wait_recv()
        rows = lands(3, s)
        relays.append(
            send(e_im.at[3:6, rows, tile, :], e_im.at[3:6, rows, 16:24, :], partner)
        )
    for s in range(2):
        y_cw[s].wait_recv()
        rows = lands(4, s)
        relays.append(send(e_cw.at[:, rows, tile, :], e_cw.at[:, rows, 16:24, :], partner))
    for h in range(2):
        for s in range(2):
            corner[h][s].wait_recv()
        x_row[h].wait_recv()
        relays.append(send(xm.at[h, :, tile, :], xm.at[h, :, 16:24, :], partner))
    for copy in y_fine + x_fine + own + relays:
        copy.wait_recv()
    local.wait()
    for copy in started:
        copy.wait_send()


COPIES = 28


def exchange(fine, wind, inc, mis):
    return pl.pallas_call(
        exchange_kernel,
        out_shape=(
            jax.ShapeDtypeStruct((5, 16, 24, 128), F32),
            jax.ShapeDtypeStruct((6, 16, 24, COLS), F32),
            jax.ShapeDtypeStruct((2, 8, 24, 128), F32),
            jax.ShapeDtypeStruct((2, VARS, LEVS, FCOLS), F32),
            jax.ShapeDtypeStruct((2, VARS, 8, 128), F32),
            jax.ShapeDtypeStruct((VARS, FROWS, FCOLS), F32),
        ),
        in_specs=[ANY] * 4,
        out_specs=(ANY,) * 6,
        scratch_shapes=[
            pltpu.VMEM((5, LEVS, FROWS, FCOLS), F32),
            pltpu.VMEM((6, ROWS, LEVS, COLS), F32),
            pltpu.VMEM((LEVS * FROWS, 128), F32),
            pltpu.VMEM((5, ROWS, LEVS, 128), F32),
            pltpu.VMEM((2, 8, LEVS, 128), F32),
            pltpu.VMEM((2, VARS, LEVS, FCOLS), F32),
            pltpu.VMEM((2, VARS, 8, 128), F32),
            pltpu.VMEM((FCOLS, 128), BF16),
            pltpu.SemaphoreType.DMA((7,)),
            pltpu.SemaphoreType.DMA,
            pltpu.SemaphoreType.DMA((COPIES,)),
            pltpu.SemaphoreType.DMA((COPIES,)),
        ],
        compiler_params=pltpu.CompilerParams(collective_id=0, has_side_effects=True),
        name="exchange",
    )(fine, wind, inc, mis)


def solve_kernel(
    fine, wind, inc, mis, e_cw, e_im, xm, fy, fx, fl,
    fine_next, gradient,
    cw, im, xv, fyv, fxv, fn, wf, q, st, sc, d1, res, a1, up, vr, lhs, fi, table, grad, out,
    sem, out_sem,
):
    gy, lev = lax.axis_index("gy"), lax.axis_index("lev")
    other = 17 * (1 - lev)
    empty = 17 * lev

    copies = [
        pltpu.make_async_copy(e_cw, cw, sem.at[0]),
        pltpu.make_async_copy(e_im, im, sem.at[1]),
        pltpu.make_async_copy(xm, xv, sem.at[2]),
    ]
    late = [
        pltpu.make_async_copy(fy, fyv, sem.at[3]),
        pltpu.make_async_copy(fx, fxv, sem.at[4]),
        pltpu.make_async_copy(wind, wf, sem.at[5]),
    ]
    for v in range(VARS):
        late.append(
            pltpu.make_async_copy(fine.at[v], fn.at[v, 1:17, 0:24, 0:FCOLS], sem.at[6 + v])
        )
    late.append(pltpu.make_async_copy(fl, fn.at[:, other, 0:24, 0:FCOLS], sem.at[9]))
    own = [
        pltpu.make_async_copy(inc, im.at[0:3, 5:11, 0:16, :], sem.at[10]),
        pltpu.make_async_copy(mis, im.at[3:6, 5:11, 0:16, :], sem.at[11]),
    ]
    for copy in copies:
        copy.start()
    for copy in late:
        copy.start()

    source = lax.broadcasted_iota(jnp.int32, (128, 512), 0)
    target = lax.broadcasted_iota(jnp.int32, (128, 512), 1)
    target = jnp.where(target < 448, target, target - 512)
    scaled = 4 * target + 10
    beneath = lax.shift_right_arithmetic(scaled, 4)
    fraction = jnp.bitwise_and(scaled, 15).astype(F32) * 0.0625
    weights = jnp.where(source == jnp.bitwise_and(beneath - 1, 127), 1.0 - fraction, 0.0)
    weights += jnp.where(source == jnp.bitwise_and(beneath, 127), fraction, 0.0)
    table[...] = weights.astype(BF16)
    for v in range(VARS):
        fn[v, empty, 0:24, 0:FCOLS] = jnp.zeros((24, FCOLS), F32)
        vr[v, pl.ds(25 * 24, 6 * 24), :] = jnp.zeros((6 * 24, 128), F32)

    lane = lax.broadcasted_iota(jnp.int32, (24, 128), 1)
    level = lax.broadcasted_iota(jnp.int32, (24, 128), 0)
    top = jnp.where(lev == 1, 15, 24)
    bottom = jnp.where(lev == 0, 0, 24)
    above = jnp.where(level == top, 0.0, 0.1).astype(F32)
    below = jnp.where(level == bottom, 0.0, 0.1).astype(F32)

    first_row = jnp.where(gy == 0, 5, 0)
    last_row = jnp.where(gy == NGY - 1, 10, 15)

    def inside(e):
        keep = jnp.logical_and(e >= first_row, e <= last_row)
        return jnp.where(keep, 1.0, 0.0).astype(F32)

    for copy in copies:
        copy.wait()
    for copy in own:
        copy.start()
    for copy in own:
        copy.wait()

    for f in range(FIELDS):
        d = DEPTH[f]
        for e in range(5 - d, 11 + d):
            if 5 <= e < 11:
                u, (at, width) = e - 5, SEG_ROW[f]
            elif e < 5:
                u, (at, width) = 6, SEG_CORNER[f, 5 - e]
            else:
                u, (at, width) = 7, SEG_CORNER[f, e - 10]
            if f < 5:
                body = cw[f, e]
            else:
                body = jnp.concatenate([im[f - 5, e], jnp.zeros((24, 32), F32)], axis=1)
            left = pltpu.roll(xv[0, u], (128 - width - at) % 128, 1)
            right = pltpu.roll(xv[1, u], (COLS - at) % 128, 1)
            halo = jnp.where(lane >= 112, left, right)
            value = jnp.where(lane < COLS, body, halo)
            if not 5 <= e < 11 and f not in (3, 4):
                value = value * inside(e)
            q[f, e] = value

    def east(x):
        return pltpu.roll(x, 127, 1)

    def west(x):
        return pltpu.roll(x, 1, 1)

    def vertical(x):
        return pltpu.roll(x, 23, 0) * above + pltpu.roll(x, 1, 0) * below

    def forward(ref, base, v, e, wu, wv):
        k = MIX[v]
        x = ref[base + v, e]
        total = (1.0 - 4.0 * k - 0.2) * x + vertical(x)
        total += (k - wu) * east(x) + (k + wu) * west(x)
        total += (k - wv) * ref[base + v, e + 1] + (k + wv) * ref[base + v, e - 1]
        return x, total

    def adjoint(ref, v, e, wu, wn, ws):
        k = MIX[v]
        x = ref[v, e]
        total = (1.0 - 4.0 * k - 0.2) * x + vertical(x)
        total += east((k + wu) * x) + west((k - wu) * x)
        total += (k + wn) * ref[v, e + 1] + (k - ws) * ref[v, e - 1]
        return x, total

    def slope(x):
        t = jnp.tanh(x)
        return t, 0.3 - 0.3 * t * t

    def winds(e):
        return 0.125 * q[3, e], 0.125 * q[4, e]

    def stage_one(e, carry):
        wu, wv = winds(e)
        keep = inside(e)
        for v in range(VARS):
            _, s = slope(q[v, e])
            sc[v, e] = s
            x, total = forward(q, 5, v, e, wu, wv)
            d1[v, e] = (total - s * x) * keep
        return carry

    lax.fori_loop(1, 15, stage_one, 0)

    def stage_path(e, carry):
        wu, wv = winds(e)
        for v in range(VARS):
            x, total = forward(q, 0, v, e, wu, wv)
            _, s = slope(total - 0.3 * jnp.tanh(x))
            st[v, e] = s
        return carry

    lax.fori_loop(2, 14, stage_path, 0)

    def stage_two(e, carry):
        wu, wv = winds(e)
        keep = inside(e)
        for v in range(VARS):
            x, total = forward(d1, 0, v, e, wu, wv)
            res[v, e] = (total - st[v, e] * x - q[8 + v, e]) * keep
        return carry

    lax.fori_loop(2, 14, stage_two, 0)

    def stage_three(e, carry):
        wu, _ = winds(e)
        keep = inside(e)
        wn, ws = 0.125 * q[4, e + 1], 0.125 * q[4, e - 1]
        for v in range(VARS):
            x, total = adjoint(res, v, e, wu, wn, ws)
            a1[v, e] = (total - st[v, e] * x) * keep
        return carry

    lax.fori_loop(3, 13, stage_three, 0)

    def stage_four(e, carry):
        wu, _ = winds(e)
        keep = inside(e)
        wn, ws = 0.125 * q[4, e + 1], 0.125 * q[4, e - 1]
        for v in range(VARS):
            x, total = adjoint(a1, v, e, wu, wn, ws)
            start = q[5 + v, e]
            slant = start + total - sc[v, e] * x
            up[v, e - 4] = (start - 0.5 * slant) * keep
            q[v, e] = slant
        return carry

    lax.fori_loop(4, 12, stage_four, 0)
    for v in range(VARS):
        for j in range(ROWS):
            grad[v, j] = q[v, 5 + j, 0:16, 0:COLS]
    grad_copy = pltpu.make_async_copy(grad, gradient, out_sem.at[3])
    grad_copy.start()

    pieces = ((0.375, 0.625, 0.0), (0.125, 0.875, 0.0), (0.0, 0.875, 0.125), (0.0, 0.625, 0.375))
    low, high = inside(4), inside(11)
    for v in range(VARS):
        rows = [up[v, e] for e in range(8)]
        for r in range(-1, 25):
            j, a = r // 4, r % 4
            c = pieces[a]
            value = c[1] * rows[j + 1]
            if c[0]:
                value += c[0] * rows[j]
            else:
                value += c[2] * rows[j + 2]
            if r == -1:
                value = value * low
            if r == 24:
                value = value * high
            vr[v, pl.ds((r % 32) * 24, 24), :] = value

    for copy in late:
        copy.wait()

    sub = lax.broadcasted_iota(jnp.int32, (8, FCOLS), 0)
    lane_edge = lax.broadcasted_iota(jnp.int32, (24, 128), 1)
    for v in range(VARS):
        for l in range(LEVS):
            lhs[pl.ds(32 * l, 32), :] = vr[v, pl.ds(l, 32, stride=24), :]
        lhs[pl.ds(512, 32), :] = vr[v, pl.ds(16 + 7 * lev, 32, stride=24), :]
        fi[...] = split_dot(lhs[...], table[...])

        def add_state(l, carry):
            base = pl.multiple_of(32 * l, 32)
            fn[v, l + 1, 0:24, 0:FCOLS] += fi[pl.ds(base, 24), 0:FCOLS]
            south = jnp.broadcast_to(fyv[0, v, pl.ds(l, 1), :] * low, (8, FCOLS))
            north = jnp.broadcast_to(fyv[1, v, pl.ds(l, 1), :] * high, (8, FCOLS))
            edge = jnp.where(sub == 0, north, jnp.where(sub == 7, south, 0.0))
            fn[v, l + 1, 24:32, 0:FCOLS] = edge + fi[pl.ds(base + 24, 8), 0:FCOLS]
            for t in range(3):
                n = 3 * l + t
                left = pltpu.roll(fxv[0, v], 127 - n, 1)
                right = pltpu.roll(fxv[1, v], lax.rem(128 - n, 128), 1)
                side = jnp.where(lane8 == 0, right, jnp.where(lane8 == 127, left, 0.0))
                fn[v, l + 1, 8 * t : 8 * t + 8, FCOLS:512] = (
                    side + fi[pl.ds(base + 8 * t, 8), FCOLS:512]
                )
            return carry

        lane8 = lane_edge[0:8]
        lax.fori_loop(0, LEVS, add_state, 0)
        fn[v, other, 0:24, 0:FCOLS] += fi[512:536, 0:FCOLS]

    outs = []
    for v in range(VARS):
        k = MIX[v]

        def step(l, carry):
            x = fn[v, l + 1, 0:24, 0:FCOLS]
            whole = fn[v, l + 1, 0:24, :]
            tall = fn[v, l + 1, :, 0:FCOLS]
            wu, wv = 0.125 * wf[0, l], 0.125 * wf[1, l]
            total = (1.0 - 4.0 * k - 0.2) * x - 0.3 * jnp.tanh(x)
            total += 0.1 * (fn[v, l, 0:24, 0:FCOLS] + fn[v, l + 2, 0:24, 0:FCOLS])
            total += (k - wu) * pltpu.roll(whole, 511, 1)[:, 0:FCOLS]
            total += (k + wu) * pltpu.roll(whole, 1, 1)[:, 0:FCOLS]
            total += (k - wv) * pltpu.roll(tall, 31, 0)[0:24]
            total += (k + wv) * pltpu.roll(tall, 1, 0)[0:24]
            out[v, l] = total
            return carry

        lax.fori_loop(0, LEVS, step, 0)
        copy = pltpu.make_async_copy(out.at[v], fine_next.at[v], out_sem.at[v])
        copy.start()
        outs.append(copy)
    for copy in outs:
        copy.wait()
    grad_copy.wait()


def solve(*args):
    line = lambda n: pltpu.VMEM((n, 16, 24, 128), F32)
    return pl.pallas_call(
        solve_kernel,
        out_shape=(
            jax.ShapeDtypeStruct((VARS, LEVS, FROWS, FCOLS), F32),
            jax.ShapeDtypeStruct((VARS, ROWS, LEVS, COLS), F32),
        ),
        in_specs=[ANY] * 10,
        out_specs=(ANY, ANY),
        scratch_shapes=[
            line(5),
            pltpu.VMEM((6, 16, 24, COLS), F32),
            pltpu.VMEM((2, 8, 24, 128), F32),
            pltpu.VMEM((2, VARS, LEVS, FCOLS), F32),
            pltpu.VMEM((2, VARS, 8, 128), F32),
            pltpu.VMEM((VARS, 18, 32, 512), F32),
            pltpu.VMEM((2, LEVS, FROWS, FCOLS), F32),
            line(FIELDS), line(3), line(3), line(3), line(3), line(3),
            pltpu.VMEM((VARS, 8, 24, 128), F32),
            pltpu.VMEM((VARS, 32 * 24, 128), F32),
            pltpu.VMEM((17 * 32, 128), F32),
            pltpu.VMEM((17 * 32, 512), F32),
            pltpu.VMEM((128, 512), BF16),
            pltpu.VMEM((VARS, ROWS, LEVS, COLS), F32),
            pltpu.VMEM((VARS, LEVS, FROWS, FCOLS), F32),
            pltpu.SemaphoreType.DMA((12,)),
            pltpu.SemaphoreType.DMA((4,)),
        ],
        name="solve",
    )(*args)


def per_device(fine_state, wind_field, increment, misfit):
    inc = jnp.transpose(increment, (0, 2, 1, 3))
    mis = jnp.transpose(misfit, (0, 2, 1, 3))
    halos = exchange(fine_state, wind_field, inc, mis)
    fine_next, gradient = solve(fine_state, wind_field, inc, mis, *halos)
    return fine_next, jnp.transpose(gradient, (0, 2, 1, 3))


def solution(mesh):
    spec = P(None, "lev", "gy", "gx")
    return jax.shard_map(
        per_device, mesh=mesh, in_specs=(spec,) * 4, out_specs=(spec, spec), check_vma=False
    )
```

time: 135 us -> 43.2 us (0.32)
  starting transfers between devices: 63.3 us -> 0 us
  Pallas kernels: 0 us -> 42.5 us
  other arithmetic: 30.7 us -> 0 us
  local copies, waits for them, and re-layouts: 22.7 us -> 0 us
  waiting for transfers between devices: 15.8 us -> 0 us
    ppermute x34 -> x0, starting transfers between devices: 63.3 us -> none  [the longest x12 30.5 us: with_halo(): lax.ppermute(first, axis, [(b, a) for a, b in up])]
    pallas_call x0 -> x2, Pallas kernels: none -> 42.5 us  [the longest x1 22.4 us: exchange(): pl.pallas_call(exchange_kernel, out_shape=(jax.ShapeDtypeStruct((5, 16, 2...]
    unnamed x15 -> x0, local copies, waits for them, and re-layouts: 19.4 us -> none
    reduce_sum x2 -> x0, other arithmetic: 18.4 us -> none  [restrict(): return jnp.mean(blocks, axis=(3, 5))]
    ppermute x34 -> x0, waiting for transfers between devices: 15.8 us -> none  [the longest x5 7.76 us: with_halo_2(): lax.ppermute(lax.slice_in_dim(block, block.shape[dim] - width, None, axis...]
    sub x5 -> x0, other arithmetic: 5.53 us -> none  [the longest x1 3.18 us: per_device(): forward_linear(new_pad, wind_field) - damping * jnp.tanh(fine_new)]
    select_n x4 -> x0, other arithmetic: 4.15 us -> none  [zero_ends(): jnp.where(jnp.logical_or(first, final), jnp.zeros_like(padded), padded)]
    slice x17 -> x0, local copies, waits for them, and re-layouts: 1.61 us -> none  [the longest x4 0.69 us: with_halo_2(): lax.slice_in_dim(block, block.shape[dim] - width, None, axis=dim)]
  transfers between devices with their start and end apart: 34 -> 0, of which waited for: 16 -> 0; matrix products, arithmetic and copies ran while one was open for 1% -> 0% of each run, Pallas kernels for 0% -> 0%
where the time goes in v1:
time: 43.2 us; the launch traced here: 43.1 us
  Pallas kernels  42.5 us (98%)
  between operations  0.64 us (1%)
    pallas_call x1, Pallas kernels, exchange(): pl.pallas_call(exchange_kernel, out_shape=(jax.ShapeDtypeStruct((5, 16, 2...  22.4 us
    pallas_call x1, Pallas kernels, solve(): pl.pallas_call(solve_kernel, out_shape=(jax.ShapeDtypeStruct((VARS, LEVS,...  20.1 us

profile of v1, /device:TPU:1, one launch (start us, length us, event | category | flops | bytes accessed | tf_op | source)
XLA Modules:
  0.0 43.1 jit_solution(1796920707698938526)
XLA Ops:
  0.6 22.4 %exchange.1 = (f32[5,16,24,128]{3,2,1,0:T(8,128)}, f32[6,16,24,96]{3,2,1,0:T(8,128)}, f32[2,8,24,128]{3,2,1,0:T(8,128)}, f32[2,3,16,384]{3,2,1,0:T(8,128)}, f32[...) custom-call(f32[3,16,24,384]{3,2,1,0:T(8,128)} %fine.3, f32[2,16,24,384]{3,2,1,0:T(8,128)} %wind.3, f32[3,6,16,96]{3,2,1,0:T(8,128)} %bitcast.3, ...), custom_call_target="tpu_custom_call" | custom-call | tf_op jit(solution)/shard_map/exchange/pallas_call | solution.py:223
  23.0 20.1 %solve.1 = (f32[3,16,24,384]{3,2,1,0:T(8,128)}, f32[3,6,16,96]{3,2,1,0:T(8,128)}) custom-call(f32[3,16,24,384]{3,2,1,0:T(8,128)} %fine.3, f32[2,16,24,384]{3,2,1,0:T(8,128)} %wind.3, f32[3,6,16,96]{3,2,1,0:T(8,128)} %bitcast.4, f32[3,6,16,96]{3,2,1,0:T(8,128)} %bitcast.6, f32[5,16,24,128]{3,2,1,0:T(8,128)} %get-tuple-element.10.e_cw, ...), custom_call_target="tpu_custom_call" | custom-call | tf_op jit(solution)/shard_map/solve/pallas_call | solution.py:516

commit v2 on v1

v2 whole, which is shorter than its diff:
```python
import functools

import jax
import jax.numpy as jnp
from jax import lax
from jax.experimental import pallas as pl
from jax.experimental.pallas import tpu as pltpu
from jax.sharding import PartitionSpec as P

MESH = pl.DeviceIdType.MESH
F32 = jnp.float32
BF16 = jnp.bfloat16
HBM = pl.BlockSpec(memory_space=pltpu.HBM)
VMEM = pl.BlockSpec(memory_space=pltpu.VMEM)

MIX = (0.05, 0.1, 0.2)
VARS, LEVS, ROWS, COLS = 3, 16, 6, 96
FROWS, FCOLS = 24, 384
NGX, NGY = 4, 16

DEPTH = (4, 4, 4, 4, 4, 5, 5, 5, 3, 3, 3)
FIELDS = len(DEPTH)


def segments_row():
    place, at = {}, 0
    for f in range(FIELDS):
        place[f] = (at, DEPTH[f])
        at += DEPTH[f]
    return place


def segments_corner():
    place, at = {}, 0
    for f in range(FIELDS):
        for k in range(1, DEPTH[f] + 1):
            place[f, k] = (at, DEPTH[f] + 1 - k)
            at += DEPTH[f] + 1 - k
    return place


SEG_ROW = segments_row()
SEG_CORNER = segments_corner()


ITEMS = [(f, k) for f in range(5, FIELDS) for k in range(1, DEPTH[f] + 1)]
EARLY = 3 * len(ITEMS) // 4
ITEMS += [(f, k) for f in range(5) for k in range(1, DEPTH[f] + 1)]
UNITS = 3 * len(ITEMS) // 4


def two_parts(x):
    high = x.astype(BF16)
    return high, (x - high.astype(F32)).astype(BF16)


def exchange_kernel(
    fine, wind, inc, mis,
    fs, wf, base, yp, cwo, imo, xm, table_a, table_b,
    half, ys, xs, fys, fy, fxs, fx, fl, table,
    load_sem, ready, send_sem, recv_sem,
):
    gx, gy, lev = lax.axis_index("gx"), lax.axis_index("gy"), lax.axis_index("lev")
    gxs = (lax.rem(gx + 1, NGX), lax.rem(gx + NGX - 1, NGX))
    gys = (lax.rem(gy + 1, NGY), lax.rem(gy + NGY - 1, NGY))
    partner = (gx, gy, 1 - lev)
    near = [(gx, gys[0], lev), (gx, gys[1], lev), (gxs[0], gy, lev), (gxs[1], gy, lev)]

    barrier = pltpu.get_barrier_semaphore()
    for device in near + [partner]:
        pl.semaphore_signal(barrier, inc=1, device_id=device, device_id_type=MESH)

    loads = [
        pltpu.make_async_copy(inc, imo.at[0:3, :, 0:16, :], load_sem.at[5]),
        pltpu.make_async_copy(mis, imo.at[3:6, :, 0:16, :], load_sem.at[6]),
    ]
    for f in range(VARS):
        loads.append(pltpu.make_async_copy(fine.at[f], fs.at[f], load_sem.at[f]))
    for f in range(2):
        loads.append(pltpu.make_async_copy(wind.at[f], wf.at[f], load_sem.at[3 + f]))
    for copy in loads:
        copy.start()

    source = lax.broadcasted_iota(jnp.int32, (FCOLS, 128), 0) // 4
    target = lax.broadcasted_iota(jnp.int32, (FCOLS, 128), 1)
    table[...] = jnp.where(source == target, 0.0625, 0.0).astype(BF16)

    started = []

    def send(src, dst, device):
        i = len(started)
        copy = pltpu.make_async_remote_copy(
            src_ref=src, dst_ref=dst, send_sem=send_sem.at[i], recv_sem=recv_sem.at[i],
            device_id=device, device_id_type=MESH,
        )
        copy.start()
        started.append(copy)
        return copy

    tile = pl.ds(pl.multiple_of((1 - lev) * 8, 8), 8)
    lane = lax.broadcasted_iota(jnp.int32, (LEVS, 128), 1)

    def unit(f, j):
        if f < 5:
            return cwo[f, j, 0:16, :]
        body = imo[f - 5, j, 0:16, :]
        return jnp.concatenate([body, jnp.zeros((LEVS, 128 - COLS), F32)], axis=1)

    def row_of(s, k):
        return ROWS - k if s == 0 else k - 1

    def pack_rows(s, start, stop):
        for g in range(start // 3, stop // 3):
            parts = [unit(f, row_of(s, k)) for f, k in ITEMS[4 * g : 4 * g + 4]]
            for m in range(3):
                rest = pltpu.roll(parts[3], 96 - 32 * m, 1)
                ys[s, 3 * g + m] = jnp.where(lane < COLS, parts[m], rest)

    loads[0].wait()
    loads[1].wait()
    for s in range(2):
        pack_rows(s, 0, EARLY)
    pl.semaphore_wait(barrier, len(near) + 1)
    for s in range(2):
        pl.semaphore_signal(ready, inc=1, device_id=near[s], device_id_type=MESH)
    y_im = [
        send(ys.at[s, 0:EARLY], yp.at[s, 0:EARLY, 0:16, :], near[s]) for s in range(2)
    ]
    own = [send(imo.at[:, :, tile, :], imo.at[:, :, 16:24, :], partner)]

    for v in range(VARS):
        loads[2 + v].wait()
        for l in range(LEVS):
            fys[0, v, l : l + 1, :] = fs[v, l, FROWS - 1 : FROWS, :]
            fys[1, v, l : l + 1, :] = fs[v, l, 0:1, :]
    y_fine = [send(fys.at[s], fy.at[s], near[s]) for s in range(2)]

    def coarsen(f, ref):
        high, low = two_parts(ref.reshape(LEVS * FROWS, FCOLS))
        half[...] = jnp.dot(high, table[...], preferred_element_type=F32) + jnp.dot(
            low, table[...], preferred_element_type=F32
        )
        for j in range(ROWS):
            total = half[pl.ds(4 * j, LEVS, stride=FROWS), :]
            for a in range(1, 4):
                total += half[pl.ds(4 * j + a, LEVS, stride=FROWS), :]
            cwo[f, j, 0:16, :] = total

    for f in range(VARS):
        coarsen(f, fs[f])
    for f in range(2):
        loads[5 + f].wait()
        coarsen(3 + f, wf[f])
    for s in range(2):
        pack_rows(s, EARLY, UNITS)
    y_cw = [
        send(ys.at[s, EARLY:UNITS], yp.at[s, EARLY:UNITS, 0:16, :], near[s])
        for s in range(2)
    ]
    own.append(send(cwo.at[:, :, tile, :], cwo.at[:, :, 16:24, :], partner))

    def packed(out, value, h, at, width):
        first = COLS - width if h == 0 else 0
        moved = pltpu.roll(value, (at - first) % 128, 1)
        return jnp.where(jnp.logical_and(lane >= at, lane < at + width), moved, out)

    zero = jnp.zeros((LEVS, 128), F32)
    for h in range(2):
        for s in range(2):
            out = zero
            for (f, k), (at, width) in SEG_CORNER.items():
                out = packed(out, unit(f, row_of(s, k)), h, at, width)
            xs[h, 6 + s] = out
    pl.semaphore_wait(ready, 2)
    corner = [
        [
            send(xs.at[h, 6 + s], xm.at[h, 6 + s, 0:16, :], (gxs[h], gys[s], lev))
            for s in range(2)
        ]
        for h in range(2)
    ]
    for h in range(2):
        for j in range(ROWS):
            out = zero
            for f, (at, width) in SEG_ROW.items():
                out = packed(out, unit(f, j), h, at, width)
            xs[h, j] = out
    x_row = [send(xs.at[h, 0:6], xm.at[h, 0:6, 0:16, :], near[2 + h]) for h in range(2)]
    edge = 15 * (1 - lev)
    fine_lev = send(fs.at[:, edge], fl, partner)

    lane8 = lax.broadcasted_iota(jnp.int32, (8, 128), 1)
    for v in range(VARS):
        outs = [jnp.zeros((8, 128), F32)] * 2
        for l in range(LEVS):
            for t in range(3):
                n = 3 * l + t
                first = pltpu.roll(fs[v, l, 8 * t : 8 * t + 8, 0:128], n, 1)
                last = pltpu.roll(fs[v, l, 8 * t : 8 * t + 8, 256:384], (n + 1) % 128, 1)
                outs[0] = jnp.where(lane8 == n, last, outs[0])
                outs[1] = jnp.where(lane8 == n, first, outs[1])
        fxs[0, v] = outs[0]
        fxs[1, v] = outs[1]
    x_fine = [send(fxs.at[h], fx.at[h], near[2 + h]) for h in range(2)]

    coarse_lane = lax.broadcasted_iota(jnp.int32, (128, FCOLS), 0)
    fine_col = lax.broadcasted_iota(jnp.int32, (128, FCOLS), 1)

    def columns(shift):
        scaled = 4 * (fine_col + shift) + 10
        beneath = lax.shift_right_arithmetic(scaled, 4)
        fraction = jnp.bitwise_and(scaled, 15).astype(F32) * 0.0625
        first = coarse_lane == jnp.bitwise_and(beneath - 1, 127)
        second = coarse_lane == jnp.bitwise_and(beneath, 127)
        return jnp.where(first, 1.0 - fraction, 0.0) + jnp.where(second, fraction, 0.0)

    middle = columns(0).astype(BF16)
    ahead, behind = columns(1), columns(-1)
    slant = (0.125 * (behind - ahead)).astype(BF16)
    around = (ahead + behind).astype(BF16)
    for part in range(2):
        rows = slice(128 * part, 128 * part + 128)
        table_a[rows, 0:FCOLS] = middle
        table_a[rows, FCOLS:] = slant
        table_b[rows, :] = middle
        table_b[slice(256 + 128 * part, 384 + 128 * part), :] = around

    row = lax.broadcasted_iota(jnp.int32, (FROWS, FCOLS), 0)
    col = lax.broadcasted_iota(jnp.int32, (FROWS, FCOLS), 1)

    def fine_step(l, carry):
        wu, wv = 0.125 * wf[0, l], 0.125 * wf[1, l]
        has_low = jnp.where(l > 0, 0.1, 0.0).astype(F32)
        has_high = jnp.where(l < LEVS - 1, 0.1, 0.0).astype(F32)
        for v in range(VARS):
            k = MIX[v]
            x = fs[v, l]
            total = (1.0 - 4.0 * k - 0.2) * x
            total += has_low * fs[v, jnp.maximum(l - 1, 0)]
            total += has_high * fs[v, jnp.minimum(l + 1, LEVS - 1)]
            total += (k - wu) * jnp.where(col == FCOLS - 1, 0.0, pltpu.roll(x, FCOLS - 1, 1))
            total += (k + wu) * jnp.where(col == 0, 0.0, pltpu.roll(x, 1, 1))
            total += (k - wv) * jnp.where(row == FROWS - 1, 0.0, pltpu.roll(x, FROWS - 1, 0))
            total += (k + wv) * jnp.where(row == 0, 0.0, pltpu.roll(x, 1, 0))
            base[v, l] = total
        return carry

    lax.fori_loop(0, LEVS, fine_step, 0)

    relays = []
    for s in range(2):
        y_im[s].wait_recv()
        relays.append(
            send(yp.at[s, 0:EARLY, tile, :], yp.at[s, 0:EARLY, 16:24, :], partner)
        )
    for copy in y_fine + x_fine + [fine_lev]:
        copy.wait_recv()

    sub8 = lax.broadcasted_iota(jnp.int32, (8, FCOLS), 0)
    not_first = jnp.where(gy == 0, 0.0, 1.0).astype(F32)
    not_last = jnp.where(gy == NGY - 1, 0.0, 1.0).astype(F32)

    def fine_edges(l, carry):
        for v in range(VARS):
            k = MIX[v]
            south = jnp.broadcast_to(fy[0, v, pl.ds(l, 1), :] * not_first, (8, FCOLS))
            north = jnp.broadcast_to(fy[1, v, pl.ds(l, 1), :] * not_last, (8, FCOLS))
            wv0, wv1 = 0.125 * wf[1, l, 0:8], 0.125 * wf[1, l, 16:24]
            base[v, l, 0:8] += jnp.where(sub8 == 0, (k + wv0) * south, 0.0)
            base[v, l, 16:24] += jnp.where(sub8 == 7, (k - wv1) * north, 0.0)
            for t in range(3):
                n = 3 * l + t
                rows = slice(8 * t, 8 * t + 8)
                left = pltpu.roll(fx[0, v], lax.rem(128 - n, 128), 1)
                right = pltpu.roll(fx[1, v], 127 - n, 1)
                wu0, wu1 = 0.125 * wf[0, l, rows, 0:128], 0.125 * wf[0, l, rows, 256:384]
                base[v, l, rows, 0:128] += jnp.where(lane8 == 0, (k + wu0) * left, 0.0)
                base[v, l, rows, 256:384] += jnp.where(lane8 == 127, (k - wu1) * right, 0.0)
        return carry

    lax.fori_loop(0, LEVS, fine_edges, 0)
    for v in range(VARS):
        base[v, edge] += 0.1 * fl[v]

    for s in range(2):
        y_cw[s].wait_recv()
        relays.append(
            send(yp.at[s, EARLY:UNITS, tile, :], yp.at[s, EARLY:UNITS, 16:24, :], partner)
        )
    for h in range(2):
        for s in range(2):
            corner[h][s].wait_recv()
        x_row[h].wait_recv()
        relays.append(send(xm.at[h, :, tile, :], xm.at[h, :, 16:24, :], partner))
    for copy in own + relays:
        copy.wait_recv()
    for copy in started:
        copy.wait_send()


COPIES = 23


def exchange(fine, wind, inc, mis):
    return pl.pallas_call(
        exchange_kernel,
        out_shape=(
            pltpu.VMEM((VARS, LEVS, FROWS, FCOLS), F32),
            pltpu.VMEM((2, LEVS, FROWS, FCOLS), F32),
            pltpu.VMEM((VARS, LEVS, FROWS, FCOLS), F32),
            pltpu.VMEM((2, UNITS, 24, 128), F32),
            pltpu.VMEM((5, ROWS, 24, 128), F32),
            pltpu.VMEM((6, ROWS, 24, COLS), F32),
            pltpu.VMEM((2, 8, 24, 128), F32),
            pltpu.VMEM((256, 2 * FCOLS), BF16),
            pltpu.VMEM((512, FCOLS), BF16),
        ),
        in_specs=[HBM] * 4,
        out_specs=(VMEM,) * 9,
        scratch_shapes=[
            pltpu.VMEM((LEVS * FROWS, 128), F32),
            pltpu.VMEM((2, UNITS, LEVS, 128), F32),
            pltpu.VMEM((2, 8, LEVS, 128), F32),
            pltpu.VMEM((2, VARS, LEVS, FCOLS), F32),
            pltpu.VMEM((2, VARS, LEVS, FCOLS), F32),
            pltpu.VMEM((2, VARS, 8, 128), F32),
            pltpu.VMEM((2, VARS, 8, 128), F32),
            pltpu.VMEM((VARS, FROWS, FCOLS), F32),
            pltpu.VMEM((FCOLS, 128), BF16),
            pltpu.SemaphoreType.DMA((7,)),
            pltpu.SemaphoreType.REGULAR,
            pltpu.SemaphoreType.DMA((COPIES,)),
            pltpu.SemaphoreType.DMA((COPIES,)),
        ],
        compiler_params=pltpu.CompilerParams(
            vmem_limit_bytes=20 << 20, collective_id=0, has_side_effects=True
        ),
        name="exchange",
    )(fine, wind, inc, mis)


def solve_kernel(
    fs, wf, base, yp, cwo, imo, xm, table_a, table_b,
    fine_next, gradient,
    q, st, sc, d1, res, a1, up, vr, lv, ly, grad, out, out_sem,
):
    gy, lev = lax.axis_index("gy"), lax.axis_index("lev")
    lane = lax.broadcasted_iota(jnp.int32, (24, 128), 1)
    level = lax.broadcasted_iota(jnp.int32, (24, 128), 0)
    top = jnp.where(lev == 1, 15, 24)
    bottom = jnp.where(lev == 0, 0, 24)
    above = jnp.where(level == top, 0.0, 0.1).astype(F32)
    below = jnp.where(level == bottom, 0.0, 0.1).astype(F32)

    first_row = jnp.where(gy == 0, 5, 0)
    last_row = jnp.where(gy == NGY - 1, 10, 15)

    def inside(e):
        keep = jnp.logical_and(e >= first_row, e <= last_row)
        return jnp.where(keep, 1.0, 0.0).astype(F32)

    def fill(f, e, body, u, at, width):
        left = pltpu.roll(xm[0, u], (128 - width - at) % 128, 1)
        right = pltpu.roll(xm[1, u], (COLS - at) % 128, 1)
        value = jnp.where(lane < COLS, body, jnp.where(lane >= 112, left, right))
        if not 5 <= e < 11 and f not in (3, 4):
            value = value * inside(e)
        q[f, e] = value

    for f in range(FIELDS):
        for j in range(ROWS):
            if f < 5:
                body = cwo[f, j]
            else:
                body = jnp.concatenate([imo[f - 5, j], jnp.zeros((24, 32), F32)], axis=1)
            fill(f, 5 + j, body, j, *SEG_ROW[f])
    for s in range(2):
        for i, (f, k) in enumerate(ITEMS):
            g, m = i // 4, i % 4
            if m < 3:
                body = yp[s, 3 * g + m]
            else:
                pieces = [pltpu.roll(yp[s, 3 * g + n], 32 + 32 * n, 1) for n in range(3)]
                body = jnp.where(
                    lane < 32, pieces[0], jnp.where(lane < 64, pieces[1], pieces[2])
                )
            fill(f, 5 - k if s == 0 else 10 + k, body, 6 + s, *SEG_CORNER[f, k])

    def east(x):
        return pltpu.roll(x, 127, 1)

    def west(x):
        return pltpu.roll(x, 1, 1)

    def vertical(x):
        return pltpu.roll(x, 23, 0) * above + pltpu.roll(x, 1, 0) * below

    def forward(ref, base, v, e, wu, wv):
        k = MIX[v]
        x = ref[base + v, e]
        total = (1.0 - 4.0 * k - 0.2) * x + vertical(x)
        total += (k - wu) * east(x) + (k + wu) * west(x)
        total += (k - wv) * ref[base + v, e + 1] + (k + wv) * ref[base + v, e - 1]
        return x, total

    def adjoint(ref, v, e, wu, wn, ws):
        k = MIX[v]
        x = ref[v, e]
        total = (1.0 - 4.0 * k - 0.2) * x + vertical(x)
        total += east((k + wu) * x) + west((k - wu) * x)
        total += (k + wn) * ref[v, e + 1] + (k - ws) * ref[v, e - 1]
        return x, total

    def slope(x):
        t = jnp.tanh(x)
        return t, 0.3 - 0.3 * t * t

    def winds(e):
        return 0.125 * q[3, e], 0.125 * q[4, e]

    def stage_one(e, carry):
        wu, wv = winds(e)
        keep = inside(e)
        for v in range(VARS):
            _, s = slope(q[v, e])
            sc[v, e] = s
            x, total = forward(q, 5, v, e, wu, wv)
            d1[v, e] = (total - s * x) * keep
        return carry

    for e in range(1, 15):
        stage_one(e, 0)

    def stage_path(e, carry):
        wu, wv = winds(e)
        for v in range(VARS):
            x, total = forward(q, 0, v, e, wu, wv)
            _, s = slope(total - 0.3 * jnp.tanh(x))
            st[v, e] = s
        return carry

    for e in range(2, 14):
        stage_path(e, 0)

    def stage_two(e, carry):
        wu, wv = winds(e)
        keep = inside(e)
        for v in range(VARS):
            x, total = forward(d1, 0, v, e, wu, wv)
            res[v, e] = (total - st[v, e] * x - q[8 + v, e]) * keep
        return carry

    for e in range(2, 14):
        stage_two(e, 0)

    def stage_three(e, carry):
        wu, _ = winds(e)
        keep = inside(e)
        wn, ws = 0.125 * q[4, e + 1], 0.125 * q[4, e - 1]
        for v in range(VARS):
            x, total = adjoint(res, v, e, wu, wn, ws)
            a1[v, e] = (total - st[v, e] * x) * keep
        return carry

    for e in range(3, 13):
        stage_three(e, 0)

    def stage_four(e, carry):
        wu, _ = winds(e)
        keep = inside(e)
        wn, ws = 0.125 * q[4, e + 1], 0.125 * q[4, e - 1]
        for v in range(VARS):
            x, total = adjoint(a1, v, e, wu, wn, ws)
            start = q[5 + v, e]
            slant = start + total - sc[v, e] * x
            up[v, e - 4] = (start - 0.5 * slant) * keep
            q[v, e] = slant
        return carry

    for e in range(4, 12):
        stage_four(e, 0)
    for v in range(VARS):
        for j in range(ROWS):
            grad[v, j] = q[v, 5 + j, 0:16, 0:COLS]
    grad_copy = pltpu.make_async_copy(grad, gradient, out_sem.at[6])
    grad_copy.start()

    pieces = ((0.375, 0.625, 0.0), (0.125, 0.875, 0.0), (0.0, 0.875, 0.125), (0.0, 0.625, 0.375))
    low, high = inside(4), inside(11)
    outs = []
    for v in range(VARS):
        k = MIX[v]
        rows = [up[v, e] for e in range(8)]

        def fine_row(r):
            j, a = r // 4, r % 4
            c = pieces[a]
            value = c[1] * rows[j + 1]
            value += c[0] * rows[j] if c[0] else c[2] * rows[j + 2]
            if r == -1:
                value = value * low
            if r == 24:
                value = value * high
            return value

        south, here = fine_row(-1), fine_row(0)
        for r in range(FROWS):
            north = fine_row(r + 1)
            mixed = ((0.8 - 4.0 * k) / k) * here + (north + south) + (1.0 / k) * vertical(here)
            at = pl.ds(24 * r, LEVS)
            vr[0, at, :] = here[0:16]
            vr[1, at, :] = mixed[0:16]
            vr[2, at, :] = 0.125 * (south - north)[0:16]
            south, here = here, north
        for l in range(LEVS):
            at = pl.ds(24 * l, 24)
            by_level = pl.ds(l, 24, stride=24)
            lv[at, 256:384], lv[at, 384:512] = two_parts(vr[0, by_level, :])
            lv[at, 0:128], lv[at, 128:256] = two_parts(vr[1, by_level, :])
            ly[at, 0:128], ly[at, 128:256] = two_parts(vr[2, by_level, :])
        for c in range(2):
            at = slice(192 * c, 192 * c + 192)
            levels = slice(8 * c, 8 * c + 8)
            shape = (8, FROWS, FCOLS)

            def dot(x, t):
                return jnp.dot(x, t, preferred_element_type=F32).reshape(shape)

            step = dot(lv[at, 256:512], table_a[:, 0:FCOLS])
            total = base[v, levels] - 0.3 * jnp.tanh(fs[v, levels] + step)
            total += k * dot(lv[at, :], table_b[...])
            total += wf[0, levels] * dot(lv[at, 256:512], table_a[:, FCOLS:])
            total += wf[1, levels] * dot(ly[at, :], table_a[:, 0:FCOLS])
            out[v, levels] = total
            copy = pltpu.make_async_copy(
                out.at[v, levels], fine_next.at[v, levels], out_sem.at[2 * v + c]
            )
            copy.start()
            outs.append(copy)
    for copy in outs:
        copy.wait()
    grad_copy.wait()


def solve(*args):
    line = lambda n: pltpu.VMEM((n, 16, 24, 128), F32)
    return pl.pallas_call(
        solve_kernel,
        out_shape=(
            jax.ShapeDtypeStruct((VARS, LEVS, FROWS, FCOLS), F32),
            jax.ShapeDtypeStruct((VARS, ROWS, LEVS, COLS), F32),
        ),
        in_specs=[VMEM] * 9,
        out_specs=(HBM, HBM),
        scratch_shapes=[
            line(FIELDS), line(3), line(3), line(3), line(3), line(3),
            pltpu.VMEM((VARS, 8, 24, 128), F32),
            pltpu.VMEM((3, 24 * 24, 128), F32),
            pltpu.VMEM((LEVS * FROWS, 512), BF16),
            pltpu.VMEM((LEVS * FROWS, 256), BF16),
            pltpu.VMEM((VARS, ROWS, LEVS, COLS), F32),
            pltpu.VMEM((VARS, LEVS, FROWS, FCOLS), F32),
            pltpu.SemaphoreType.DMA((7,)),
        ],
        compiler_params=pltpu.CompilerParams(vmem_limit_bytes=40 << 20),
        name="solve",
    )(*args)


def per_device(fine_state, wind_field, increment, misfit):
    inc = jnp.transpose(increment, (0, 2, 1, 3))
    mis = jnp.transpose(misfit, (0, 2, 1, 3))
    held = [pltpu.with_memory_space_constraint(x, pltpu.HBM) for x in (fine_state, wind_field, inc, mis)]
    fine_next, gradient = solve(*exchange(*held))
    return fine_next, jnp.transpose(gradient, (0, 2, 1, 3))


def solution(mesh):
    spec = P(None, "lev", "gy", "gx")
    return jax.shard_map(
        per_device, mesh=mesh, in_specs=(spec,) * 4, out_specs=(spec, spec), check_vma=False
    )
```

time: 43.2 us -> 27.3 us (0.63)
  Pallas kernels: 42.5 us -> 26.6 us
    pallas_call x1, Pallas kernels: 20.1 us -> 5.65 us  [solve(): pl.pallas_call(solve_kernel, out_shape=(jax.ShapeDtypeStruct((VARS, LEVS,...]
    pallas_call x1, Pallas kernels: 22.4 us -> 20.9 us  [exchange(): pl.pallas_call(exchange_kernel, out_shape=(pltpu.VMEM((VARS, LEVS, FROWS,...]
where the time goes in v2:
time: 27.3 us; the launch traced here: 27.2 us
  Pallas kernels  26.6 us (97%)
  between operations  0.64 us (2%)
    pallas_call x1, Pallas kernels, exchange(): pl.pallas_call(exchange_kernel, out_shape=(pltpu.VMEM((VARS, LEVS, FROWS,...  20.9 us
    pallas_call x1, Pallas kernels, solve(): pl.pallas_call(solve_kernel, out_shape=(jax.ShapeDtypeStruct((VARS, LEVS,...  5.65 us

profile of v2, /device:TPU:1, one launch (start us, length us, event | category | flops | bytes accessed | tf_op | source)
XLA Modules:
  0.0 27.2 jit_solution(7049717358993486759)
XLA Ops:
  0.6 20.9 %exchange.1 = (f32[3,16,24,384]{3,2,1,0:T(8,128)S(1)}, f32[2,16,24,384]{3,2,1,0:T(8,128)S(1)}, f32[3,16,24,384]{3,2,1,0:T(8,128)S(1)}, f32[2,33,24,128]{3,2,1,0:...) custom-call(f32[3,16,24,384]{3,2,1,0:T(8,128)} %fine.1, ...), custom_call_target="tpu_custom_call" | custom-call | tf_op jit(solution)/shard_map/exchange/pallas_call | solution.py:305
  21.6 5.6 %solve.1 = (f32[3,16,24,384]{3,2,1,0:T(8,128)}, f32[3,6,16,96]{3,2,1,0:T(8,128)}) custom-call(f32[3,16,24,384]{3,2,1,0:T(8,128)S(1)} %get-tuple-element.13.fs, f32[2,16,24,384]{3,2,1,0:T(8,128)S(1)} %get-tuple-element.14.wf, f32[3,16,24,384]{3,2,1,0:T(8,128)S(1)} %get-tuple-element.15.base, f32[2,33,24,128]{3,2,1,0:T(8,128)S(1)} %get-tuple-element.16.yp, ...), custom_call_target="tpu_custom_call" | custom-call | tf_op jit(solution)/shard_map/solve/pallas_call | solution.py:547

commit v3 on v2

--- a/solution.py
+++ b/solution.py
@@ -58,7 +58,7 @@
     fine, wind, inc, mis,
     fs, wf, base, yp, cwo, imo, xm, table_a, table_b,
     half, ys, xs, fys, fy, fxs, fx, fl, table,
-    load_sem, ready, send_sem, recv_sem,
+    load_sem, answer, ready, send_sem, recv_sem,
 ):
     gx, gy, lev = lax.axis_index("gx"), lax.axis_index("gy"), lax.axis_index("lev")
     gxs = (lax.rem(gx + 1, NGX), lax.rem(gx + NGX - 1, NGX))
@@ -66,9 +66,24 @@
     partner = (gx, gy, 1 - lev)
     near = [(gx, gys[0], lev), (gx, gys[1], lev), (gxs[0], gy, lev), (gxs[1], gy, lev)]
 
+    has_next, has_last = gy < NGY - 1, gy > 0
+    going, coming = (has_next, has_last), (has_last, has_next)
+    rows_near = has_next.astype(jnp.int32) + has_last.astype(jnp.int32)
+
+    def signal(semaphore, device, condition=None):
+        def act():
+            pl.semaphore_signal(semaphore, inc=1, device_id=device, device_id_type=MESH)
+
+        act() if condition is None else pl.when(condition)(act)
+
     barrier = pltpu.get_barrier_semaphore()
-    for device in near + [partner]:
-        pl.semaphore_signal(barrier, inc=1, device_id=device, device_id_type=MESH)
+    for s in range(2):
+        signal(barrier, near[s], going[s])
+    signal(barrier, partner)
+    signal(barrier, near[2], gx < NGX - 1)
+    signal(barrier, near[3], gx == 0)
+    greeted = (gx > 0).astype(jnp.int32) + (gx == NGX - 1).astype(jnp.int32)
+    answered = (gx < NGX - 1).astype(jnp.int32) + (gx == 0).astype(jnp.int32)
 
     loads = [
         pltpu.make_async_copy(inc, imo.at[0:3, :, 0:16, :], load_sem.at[5]),
@@ -87,15 +102,28 @@
 
     started = []
 
-    def send(src, dst, device):
+    def when(condition, act):
+        act() if condition is None else pl.when(condition)(act)
+
+    def send(src, dst, device, goes=None, comes=None):
         i = len(started)
         copy = pltpu.make_async_remote_copy(
             src_ref=src, dst_ref=dst, send_sem=send_sem.at[i], recv_sem=recv_sem.at[i],
             device_id=device, device_id_type=MESH,
         )
-        copy.start()
-        started.append(copy)
-        return copy
+        when(goes, copy.start)
+        started.append((copy, goes))
+        return copy, comes
+
+    def arrive(message):
+        when(message[1], message[0].wait_recv)
+
+    def send_row(src, dst, s):
+        return send(src, dst, near[s], going[s], coming[s])
+
+    def relay(ref, at, comes=None):
+        dst = ref.at[(*at, slice(16, 24), slice(None))]
+        return send(ref.at[(*at, tile, slice(None))], dst, partner, comes, comes)
 
     tile = pl.ds(pl.multiple_of((1 - lev) * 8, 8), 8)
     lane = lax.broadcasted_iota(jnp.int32, (LEVS, 128), 1)
@@ -120,20 +148,11 @@
     loads[1].wait()
     for s in range(2):
         pack_rows(s, 0, EARLY)
-    pl.semaphore_wait(barrier, len(near) + 1)
-    for s in range(2):
-        pl.semaphore_signal(ready, inc=1, device_id=near[s], device_id_type=MESH)
-    y_im = [
-        send(ys.at[s, 0:EARLY], yp.at[s, 0:EARLY, 0:16, :], near[s]) for s in range(2)
-    ]
+    pl.semaphore_wait(barrier, rows_near + greeted + 1)
+    y_im = [send_row(ys.at[s, 0:EARLY], yp.at[s, 0:EARLY, 0:16, :], s) for s in range(2)]
+    signal(answer, near[3], gx > 0)
+    signal(answer, near[2], gx == NGX - 1)
     own = [send(imo.at[:, :, tile, :], imo.at[:, :, 16:24, :], partner)]
-
-    for v in range(VARS):
-        loads[2 + v].wait()
-        for l in range(LEVS):
-            fys[0, v, l : l + 1, :] = fs[v, l, FROWS - 1 : FROWS, :]
-            fys[1, v, l : l + 1, :] = fs[v, l, 0:1, :]
-    y_fine = [send(fys.at[s], fy.at[s], near[s]) for s in range(2)]
 
     def coarsen(f, ref):
         high, low = two_parts(ref.reshape(LEVS * FROWS, FCOLS))
@@ -147,6 +166,7 @@
             cwo[f, j, 0:16, :] = total
 
     for f in range(VARS):
+        loads[2 + f].wait()
         coarsen(f, fs[f])
     for f in range(2):
         loads[5 + f].wait()
@@ -154,8 +174,7 @@
     for s in range(2):
         pack_rows(s, EARLY, UNITS)
     y_cw = [
-        send(ys.at[s, EARLY:UNITS], yp.at[s, EARLY:UNITS, 0:16, :], near[s])
-        for s in range(2)
+        send_row(ys.at[s, EARLY:UNITS], yp.at[s, EARLY:UNITS, 0:16, :], s) for s in range(2)
     ]
     own.append(send(cwo.at[:, :, tile, :], cwo.at[:, :, 16:24, :], partner))
 
@@ -171,23 +190,24 @@
             for (f, k), (at, width) in SEG_CORNER.items():
                 out = packed(out, unit(f, row_of(s, k)), h, at, width)
             xs[h, 6 + s] = out
-    pl.semaphore_wait(ready, 2)
-    corner = [
-        [
-            send(xs.at[h, 6 + s], xm.at[h, 6 + s, 0:16, :], (gxs[h], gys[s], lev))
-            for s in range(2)
-        ]
-        for h in range(2)
-    ]
     for h in range(2):
         for j in range(ROWS):
             out = zero
             for f, (at, width) in SEG_ROW.items():
                 out = packed(out, unit(f, j), h, at, width)
             xs[h, j] = out
+    pl.when(answered > 0)(lambda: pl.semaphore_wait(answer, answered))
+    for s in range(2):
+        signal(ready, near[s], going[s])
     x_row = [send(xs.at[h, 0:6], xm.at[h, 0:6, 0:16, :], near[2 + h]) for h in range(2)]
     edge = 15 * (1 - lev)
     fine_lev = send(fs.at[:, edge], fl, partner)
+
+    for v in range(VARS):
+        for l in range(LEVS):
+            fys[0, v, l : l + 1, :] = fs[v, l, FROWS - 1 : FROWS, :]
+            fys[1, v, l : l + 1, :] = fs[v, l, 0:1, :]
+    y_fine = [send_row(fys.at[s], fy.at[s], s) for s in range(2)]
 
     lane8 = lax.broadcasted_iota(jnp.int32, (8, 128), 1)
     for v in range(VARS):
@@ -202,6 +222,17 @@
         fxs[0, v] = outs[0]
         fxs[1, v] = outs[1]
     x_fine = [send(fxs.at[h], fx.at[h], near[2 + h]) for h in range(2)]
+    pl.semaphore_wait(ready, rows_near)
+    corner = [
+        [
+            send(
+                xs.at[h, 6 + s], xm.at[h, 6 + s, 0:16, :], (gxs[h], gys[s], lev),
+                going[s], coming[s],
+            )
+            for s in range(2)
+        ]
+        for h in range(2)
+    ]
 
     coarse_lane = lax.broadcasted_iota(jnp.int32, (128, FCOLS), 0)
     fine_col = lax.broadcasted_iota(jnp.int32, (128, FCOLS), 1)
@@ -249,25 +280,14 @@
 
     relays = []
     for s in range(2):
-        y_im[s].wait_recv()
-        relays.append(
-            send(yp.at[s, 0:EARLY, tile, :], yp.at[s, 0:EARLY, 16:24, :], partner)
-        )
-    for copy in y_fine + x_fine + [fine_lev]:
-        copy.wait_recv()
-
-    sub8 = lax.broadcasted_iota(jnp.int32, (8, FCOLS), 0)
-    not_first = jnp.where(gy == 0, 0.0, 1.0).astype(F32)
-    not_last = jnp.where(gy == NGY - 1, 0.0, 1.0).astype(F32)
-
-    def fine_edges(l, carry):
+        arrive(y_im[s])
+        relays.append(relay(yp, (s, slice(0, EARLY)), coming[s]))
+    for message in x_fine + [fine_lev]:
+        arrive(message)
+
+    def fine_columns(l, carry):
         for v in range(VARS):
             k = MIX[v]
-            south = jnp.broadcast_to(fy[0, v, pl.ds(l, 1), :] * not_first, (8, FCOLS))
-            north = jnp.broadcast_to(fy[1, v, pl.ds(l, 1), :] * not_last, (8, FCOLS))
-            wv0, wv1 = 0.125 * wf[1, l, 0:8], 0.125 * wf[1, l, 16:24]
-            base[v, l, 0:8] += jnp.where(sub8 == 0, (k + wv0) * south, 0.0)
-            base[v, l, 16:24] += jnp.where(sub8 == 7, (k - wv1) * north, 0.0)
             for t in range(3):
                 n = 3 * l + t
                 rows = slice(8 * t, 8 * t + 8)
@@ -278,27 +298,44 @@
                 base[v, l, rows, 256:384] += jnp.where(lane8 == 127, (k - wu1) * right, 0.0)
         return carry
 
-    lax.fori_loop(0, LEVS, fine_edges, 0)
+    lax.fori_loop(0, LEVS, fine_columns, 0)
     for v in range(VARS):
         base[v, edge] += 0.1 * fl[v]
 
+    for h in range(2):
+        arrive(x_row[h])
+        relays.append(relay(xm, (h, slice(0, 6))))
     for s in range(2):
-        y_cw[s].wait_recv()
-        relays.append(
-            send(yp.at[s, EARLY:UNITS, tile, :], yp.at[s, EARLY:UNITS, 16:24, :], partner)
-        )
+        arrive(y_cw[s])
+        relays.append(relay(yp, (s, slice(EARLY, UNITS)), coming[s]))
     for h in range(2):
         for s in range(2):
-            corner[h][s].wait_recv()
-        x_row[h].wait_recv()
-        relays.append(send(xm.at[h, :, tile, :], xm.at[h, :, 16:24, :], partner))
-    for copy in own + relays:
-        copy.wait_recv()
-    for copy in started:
-        copy.wait_send()
-
-
-COPIES = 23
+            arrive(corner[h][s])
+            relays.append(relay(xm, (h, 6 + s), coming[s]))
+
+    for message in y_fine:
+        arrive(message)
+    sub8 = lax.broadcasted_iota(jnp.int32, (8, FCOLS), 0)
+
+    def fine_rows(l, carry):
+        for v in range(VARS):
+            k = MIX[v]
+            south = jnp.broadcast_to(fy[0, v, pl.ds(l, 1), :], (8, FCOLS))
+            north = jnp.broadcast_to(fy[1, v, pl.ds(l, 1), :], (8, FCOLS))
+            south = jnp.where(jnp.logical_and(sub8 == 0, gy > 0), south, 0.0)
+            north = jnp.where(jnp.logical_and(sub8 == 7, gy < NGY - 1), north, 0.0)
+            base[v, l, 0:8] += (k + 0.125 * wf[1, l, 0:8]) * south
+            base[v, l, 16:24] += (k - 0.125 * wf[1, l, 16:24]) * north
+        return carry
+
+    lax.fori_loop(0, LEVS, fine_rows, 0)
+    for message in own + relays:
+        arrive(message)
+    for copy, goes in started:
+        when(goes, copy.wait_send)
+
+
+COPIES = 27
 
 
 def exchange(fine, wind, inc, mis):
@@ -329,6 +366,7 @@
             pltpu.VMEM((FCOLS, 128), BF16),
             pltpu.SemaphoreType.DMA((7,)),
             pltpu.SemaphoreType.REGULAR,
+            pltpu.SemaphoreType.REGULAR,
             pltpu.SemaphoreType.DMA((COPIES,)),
             pltpu.SemaphoreType.DMA((COPIES,)),
         ],
@@ -355,16 +393,18 @@
     first_row = jnp.where(gy == 0, 5, 0)
     last_row = jnp.where(gy == NGY - 1, 10, 15)
 
+    def within(e):
+        return jnp.logical_and(e >= first_row, e <= last_row)
+
     def inside(e):
-        keep = jnp.logical_and(e >= first_row, e <= last_row)
-        return jnp.where(keep, 1.0, 0.0).astype(F32)
+        return jnp.where(within(e), 1.0, 0.0).astype(F32)
 
     def fill(f, e, body, u, at, width):
         left = pltpu.roll(xm[0, u], (128 - width - at) % 128, 1)
         right = pltpu.roll(xm[1, u], (COLS - at) % 128, 1)
         value = jnp.where(lane < COLS, body, jnp.where(lane >= 112, left, right))
-        if not 5 <= e < 11 and f not in (3, 4):
-            value = value * inside(e)
+        if not 5 <= e < 11:
+            value = jnp.where(within(e), value, 0.0)
         q[f, e] = value
 
     for f in range(FIELDS):

time: 27.3 us -> 24.3 us (0.89)
  the two profiles are of different devices: /device:TPU:1 before, /device:TPU:25 now
where the time goes in v3:
time: 24.3 us; the launch traced here: 24.2 us
  Pallas kernels  23.5 us (97%)
  between operations  0.64 us (3%)
    pallas_call x1, Pallas kernels, exchange(): pl.pallas_call(exchange_kernel, out_shape=(pltpu.VMEM((VARS, LEVS, FROWS,...  17.9 us
    pallas_call x1, Pallas kernels, solve(): pl.pallas_call(solve_kernel, out_shape=(jax.ShapeDtypeStruct((VARS, LEVS,...  5.64 us

profile of v3, /device:TPU:25, one launch (start us, length us, event | category | flops | bytes accessed | tf_op | source)
XLA Modules:
  0.0 24.2 jit_solution(12519529541893145589)
XLA Ops:
  0.6 17.9 %exchange.1 = (f32[3,16,24,384]{3,2,1,0:T(8,128)S(1)}, f32[2,16,24,384]{3,2,1,0:T(8,128)S(1)}, f32[3,16,24,384]{3,2,1,0:T(8,128)S(1)}, f32[2,33,24,128]{3,2,1,0:...) custom-call(f32[3,16,24,384]{3,2,1,0:T(8,128)} %fine.1, ...), custom_call_target="tpu_custom_call" | custom-call | tf_op jit(solution)/shard_map/exchange/pallas_call | solution.py:342
  18.5 5.6 %solve.1 = (f32[3,16,24,384]{3,2,1,0:T(8,128)}, f32[3,6,16,96]{3,2,1,0:T(8,128)}) custom-call(f32[3,16,24,384]{3,2,1,0:T(8,128)S(1)} %get-tuple-element.13.fs, f32[2,16,24,384]{3,2,1,0:T(8,128)S(1)} %get-tuple-element.14.wf, f32[3,16,24,384]{3,2,1,0:T(8,128)S(1)} %get-tuple-element.15.base, f32[2,33,24,128]{3,2,1,0:T(8,128)S(1)} %get-tuple-element.16.yp, ...), custom_call_target="tpu_custom_call" | custom-call | tf_op jit(solution)/shard_map/solve/pallas_call | solution.py:587

commit v4 on v3

--- a/solution.py
+++ b/solution.py
@@ -58,7 +58,7 @@
     fine, wind, inc, mis,
     fs, wf, base, yp, cwo, imo, xm, table_a, table_b,
     half, ys, xs, fys, fy, fxs, fx, fl, table,
-    load_sem, answer, ready, send_sem, recv_sem,
+    load_sem, answer, known, ready, send_sem, recv_sem,
 ):
     gx, gy, lev = lax.axis_index("gx"), lax.axis_index("gy"), lax.axis_index("lev")
     gxs = (lax.rem(gx + 1, NGX), lax.rem(gx + NGX - 1, NGX))
@@ -98,22 +98,33 @@
 
     source = lax.broadcasted_iota(jnp.int32, (FCOLS, 128), 0) // 4
     target = lax.broadcasted_iota(jnp.int32, (FCOLS, 128), 1)
-    table[...] = jnp.where(source == target, 0.0625, 0.0).astype(BF16)
+    mean = jnp.where(source == target, 0.0625, 0.0).astype(BF16)
+    table[0:FCOLS] = mean
+    table[FCOLS : 2 * FCOLS] = mean
 
     started = []
 
     def when(condition, act):
         act() if condition is None else pl.when(condition)(act)
 
-    def send(src, dst, device, goes=None, comes=None):
+    def prepare(src, dst, device, goes=None, comes=None):
         i = len(started)
         copy = pltpu.make_async_remote_copy(
             src_ref=src, dst_ref=dst, send_sem=send_sem.at[i], recv_sem=recv_sem.at[i],
             device_id=device, device_id_type=MESH,
         )
-        when(goes, copy.start)
         started.append((copy, goes))
-        return copy, comes
+        return copy, comes, goes
+
+    def send(*args):
+        message = prepare(*args)
+        when(message[2], message[0].start)
+        return message
+
+    def start(message, condition):
+        goes = message[2]
+        both = condition if goes is None else jnp.logical_and(condition, goes)
+        pl.when(both)(message[0].start)
 
     def arrive(message):
         when(message[1], message[0].wait_recv)
@@ -148,36 +159,33 @@
     loads[1].wait()
     for s in range(2):
         pack_rows(s, 0, EARLY)
-    pl.semaphore_wait(barrier, rows_near + greeted + 1)
-    y_im = [send_row(ys.at[s, 0:EARLY], yp.at[s, 0:EARLY, 0:16, :], s) for s in range(2)]
-    signal(answer, near[3], gx > 0)
-    signal(answer, near[2], gx == NGX - 1)
-    own = [send(imo.at[:, :, tile, :], imo.at[:, :, 16:24, :], partner)]
-
-    def coarsen(f, ref):
-        high, low = two_parts(ref.reshape(LEVS * FROWS, FCOLS))
-        half[...] = jnp.dot(high, table[...], preferred_element_type=F32) + jnp.dot(
-            low, table[...], preferred_element_type=F32
-        )
+    def coarsen(f):
+        loads[2 + f].wait()
+        ref = fs[f] if f < VARS else wf[f - VARS]
+        parts = jnp.concatenate(two_parts(ref.reshape(LEVS * FROWS, FCOLS)), axis=1)
+        half[...] = jnp.dot(parts, table[...], preferred_element_type=F32)
         for j in range(ROWS):
             total = half[pl.ds(4 * j, LEVS, stride=FROWS), :]
             for a in range(1, 4):
                 total += half[pl.ds(4 * j + a, LEVS, stride=FROWS), :]
             cwo[f, j, 0:16, :] = total
 
-    for f in range(VARS):
-        loads[2 + f].wait()
-        coarsen(f, fs[f])
-    for f in range(2):
-        loads[5 + f].wait()
-        coarsen(3 + f, wf[f])
-    for s in range(2):
-        pack_rows(s, EARLY, UNITS)
-    y_cw = [
-        send_row(ys.at[s, EARLY:UNITS], yp.at[s, EARLY:UNITS, 0:16, :], s) for s in range(2)
-    ]
-    own.append(send(cwo.at[:, :, tile, :], cwo.at[:, :, 16:24, :], partner))
-
+    coarsen(0)
+    coarsen(1)
+    pl.semaphore_wait(barrier, rows_near + greeted + 1)
+    y_im = [send_row(ys.at[s, 0:EARLY], yp.at[s, 0:EARLY, 0:16, :], s) for s in range(2)]
+    signal(answer, near[3], gx > 0)
+    signal(answer, near[2], gx == NGX - 1)
+    early, late = answered == 0, answered > 0
+    signal(known, partner, early)
+    own = [send(imo.at[:, :, tile, :], imo.at[:, :, 16:24, :], partner)]
+
+    coarsen(2)
+    pl.when(early)(lambda: pl.semaphore_wait(known, 1))
+    for s in range(2):
+        signal(ready, near[s], jnp.logical_and(going[s], early))
+    coarsen(3)
+    coarsen(4)
     def packed(out, value, h, at, width):
         first = COLS - width if h == 0 else 0
         moved = pltpu.roll(value, (at - first) % 128, 1)
@@ -190,16 +198,46 @@
             for (f, k), (at, width) in SEG_CORNER.items():
                 out = packed(out, unit(f, row_of(s, k)), h, at, width)
             xs[h, 6 + s] = out
+    def prepare_pair(h, at, device, goes=None, comes=None):
+        there = xm.at[h, at]
+        spread = (slice(None),) * (len(there.shape) - 2)
+        low, adjacent = (*spread, slice(0, 16)), (*spread, slice(16, 24))
+        cross = (*device[:2], 1 - lev)
+        return [
+            prepare(xs.at[h, at], there.at[low], device, goes, comes),
+            prepare(xs.at[h, at].at[(*spread, tile)], there.at[adjacent], cross, goes, comes),
+        ]
+
+    corner = []
+    for h in range(2):
+        for s in range(2):
+            device = (gxs[h], gys[s], lev)
+            corner += prepare_pair(h, 6 + s, device, going[s], coming[s])
+
+    def send_corners(condition):
+        pl.when(condition)(lambda: pl.semaphore_wait(ready, rows_near))
+        for message in corner:
+            start(message, condition)
+
+    send_corners(early)
+    for s in range(2):
+        pack_rows(s, EARLY, UNITS)
+    y_cw = [
+        send_row(ys.at[s, EARLY:UNITS], yp.at[s, EARLY:UNITS, 0:16, :], s) for s in range(2)
+    ]
+    own.append(send(cwo.at[:, :, tile, :], cwo.at[:, :, 16:24, :], partner))
+
     for h in range(2):
         for j in range(ROWS):
             out = zero
             for f, (at, width) in SEG_ROW.items():
                 out = packed(out, unit(f, j), h, at, width)
             xs[h, j] = out
-    pl.when(answered > 0)(lambda: pl.semaphore_wait(answer, answered))
-    for s in range(2):
-        signal(ready, near[s], going[s])
-    x_row = [send(xs.at[h, 0:6], xm.at[h, 0:6, 0:16, :], near[2 + h]) for h in range(2)]
+    x_row = []
+    for h in range(2):
+        x_row += prepare_pair(h, slice(0, 6), near[2 + h])
+    for message in x_row:
+        start(message, early)
     edge = 15 * (1 - lev)
     fine_lev = send(fs.at[:, edge], fl, partner)
 
@@ -221,18 +259,9 @@
                 outs[1] = jnp.where(lane8 == n, first, outs[1])
         fxs[0, v] = outs[0]
         fxs[1, v] = outs[1]
-    x_fine = [send(fxs.at[h], fx.at[h], near[2 + h]) for h in range(2)]
-    pl.semaphore_wait(ready, rows_near)
-    corner = [
-        [
-            send(
-                xs.at[h, 6 + s], xm.at[h, 6 + s, 0:16, :], (gxs[h], gys[s], lev),
-                going[s], coming[s],
-            )
-            for s in range(2)
-        ]
-        for h in range(2)
-    ]
+    x_fine = [prepare(fxs.at[h], fx.at[h], near[2 + h]) for h in range(2)]
+    for message in x_fine:
+        start(message, early)
 
     coarse_lane = lax.broadcasted_iota(jnp.int32, (128, FCOLS), 0)
     fine_col = lax.broadcasted_iota(jnp.int32, (128, FCOLS), 1)
@@ -276,12 +305,25 @@
             base[v, l] = total
         return carry
 
-    lax.fori_loop(0, LEVS, fine_step, 0)
+    lax.fori_loop(0, 5, fine_step, 0)
+    pl.when(late)(lambda: pl.semaphore_wait(answer, answered))
+    signal(known, partner, late)
+    pl.when(late)(lambda: pl.semaphore_wait(known, 1))
+    for s in range(2):
+        signal(ready, near[s], jnp.logical_and(going[s], late))
+    for message in x_row + x_fine:
+        start(message, late)
+    lax.fori_loop(5, 10, fine_step, 0)
+    send_corners(late)
+    lax.fori_loop(10, LEVS, fine_step, 0)
 
     relays = []
     for s in range(2):
         arrive(y_im[s])
         relays.append(relay(yp, (s, slice(0, EARLY)), coming[s]))
+    for s in range(2):
+        arrive(y_cw[s])
+        relays.append(relay(yp, (s, slice(EARLY, UNITS)), coming[s]))
     for message in x_fine + [fine_lev]:
         arrive(message)
 
@@ -302,17 +344,6 @@
     for v in range(VARS):
         base[v, edge] += 0.1 * fl[v]
 
-    for h in range(2):
-        arrive(x_row[h])
-        relays.append(relay(xm, (h, slice(0, 6))))
-    for s in range(2):
-        arrive(y_cw[s])
-        relays.append(relay(yp, (s, slice(EARLY, UNITS)), coming[s]))
-    for h in range(2):
-        for s in range(2):
-            arrive(corner[h][s])
-            relays.append(relay(xm, (h, 6 + s), coming[s]))
-
     for message in y_fine:
         arrive(message)
     sub8 = lax.broadcasted_iota(jnp.int32, (8, FCOLS), 0)
@@ -329,7 +360,7 @@
         return carry
 
     lax.fori_loop(0, LEVS, fine_rows, 0)
-    for message in own + relays:
+    for message in own + relays + x_row + corner:
         arrive(message)
     for copy, goes in started:
         when(goes, copy.wait_send)
@@ -363,8 +394,9 @@
             pltpu.VMEM((2, VARS, 8, 128), F32),
             pltpu.VMEM((2, VARS, 8, 128), F32),
             pltpu.VMEM((VARS, FROWS, FCOLS), F32),
-            pltpu.VMEM((FCOLS, 128), BF16),
+            pltpu.VMEM((2 * FCOLS, 128), BF16),
             pltpu.SemaphoreType.DMA((7,)),
+            pltpu.SemaphoreType.REGULAR,
             pltpu.SemaphoreType.REGULAR,
             pltpu.SemaphoreType.REGULAR,
             pltpu.SemaphoreType.DMA((COPIES,)),

time: 24.3 us -> 22.2 us (0.914)
  Pallas kernels: 23.5 us -> 21.5 us
    pallas_call x1, Pallas kernels: 17.9 us -> 15.8 us  [exchange(): pl.pallas_call(exchange_kernel, out_shape=(pltpu.VMEM((VARS, LEVS, FROWS,...]
where the time goes in v4:
time: 22.2 us; the launch traced here: 22.1 us
  Pallas kernels  21.5 us (97%)
  between operations  0.64 us (3%)
    pallas_call x1, Pallas kernels, exchange(): pl.pallas_call(exchange_kernel, out_shape=(pltpu.VMEM((VARS, LEVS, FROWS,...  15.8 us
    pallas_call x1, Pallas kernels, solve(): pl.pallas_call(solve_kernel, out_shape=(jax.ShapeDtypeStruct((VARS, LEVS,...  5.65 us

profile of v4, /device:TPU:25, one launch (start us, length us, event | category | flops | bytes accessed | tf_op | source)
XLA Modules:
  0.0 22.1 jit_solution(9276130312862516094)
XLA Ops:
  0.6 15.8 %exchange.1 = (f32[3,16,24,384]{3,2,1,0:T(8,128)S(1)}, f32[2,16,24,384]{3,2,1,0:T(8,128)S(1)}, f32[3,16,24,384]{3,2,1,0:T(8,128)S(1)}, f32[2,33,24,128]{3,2,1,0:...) custom-call(f32[3,16,24,384]{3,2,1,0:T(8,128)} %fine.1, ...), custom_call_target="tpu_custom_call" | custom-call | tf_op jit(solution)/shard_map/exchange/pallas_call | solution.py:373
  16.4 5.6 %solve.1 = (f32[3,16,24,384]{3,2,1,0:T(8,128)}, f32[3,6,16,96]{3,2,1,0:T(8,128)}) custom-call(f32[3,16,24,384]{3,2,1,0:T(8,128)S(1)} %get-tuple-element.13.fs, f32[2,16,24,384]{3,2,1,0:T(8,128)S(1)} %get-tuple-element.14.wf, f32[3,16,24,384]{3,2,1,0:T(8,128)S(1)} %get-tuple-element.15.base, f32[2,33,24,128]{3,2,1,0:T(8,128)S(1)} %get-tuple-element.16.yp, ...), custom_call_target="tpu_custom_call" | custom-call | tf_op jit(solution)/shard_map/solve/pallas_call | solution.py:619

commit v5 on v4

--- a/solution.py
+++ b/solution.py
@@ -177,6 +177,7 @@
     signal(answer, near[3], gx > 0)
     signal(answer, near[2], gx == NGX - 1)
     early, late = answered == 0, answered > 0
+    between, lowest = jnp.logical_and(late, gx > 0), gx == 0
     signal(known, partner, early)
     own = [send(imo.at[:, :, tile, :], imo.at[:, :, 16:24, :], partner)]
 
@@ -220,6 +221,14 @@
             start(message, condition)
 
     send_corners(early)
+
+    def hear(condition):
+        pl.when(condition)(lambda: pl.semaphore_wait(answer, answered))
+        signal(known, partner, condition)
+        pl.when(condition)(lambda: pl.semaphore_wait(known, 1))
+        for s in range(2):
+            signal(ready, near[s], jnp.logical_and(going[s], condition))
+
     for s in range(2):
         pack_rows(s, EARLY, UNITS)
     y_cw = [
@@ -236,8 +245,9 @@
     x_row = []
     for h in range(2):
         x_row += prepare_pair(h, slice(0, 6), near[2 + h])
+    hear(between)
     for message in x_row:
-        start(message, early)
+        start(message, gx > 0)
     edge = 15 * (1 - lev)
     fine_lev = send(fs.at[:, edge], fl, partner)
 
@@ -245,7 +255,11 @@
         for l in range(LEVS):
             fys[0, v, l : l + 1, :] = fs[v, l, FROWS - 1 : FROWS, :]
             fys[1, v, l : l + 1, :] = fs[v, l, 0:1, :]
-    y_fine = [send_row(fys.at[s], fy.at[s], s) for s in range(2)]
+    y_fine = [
+        prepare(fys.at[s], fy.at[s], near[s], going[s], coming[s]) for s in range(2)
+    ]
+    for message in y_fine:
+        start(message, jnp.logical_or(early, lowest))
 
     lane8 = lax.broadcasted_iota(jnp.int32, (8, 128), 1)
     for v in range(VARS):
@@ -261,7 +275,7 @@
         fxs[1, v] = outs[1]
     x_fine = [prepare(fxs.at[h], fx.at[h], near[2 + h]) for h in range(2)]
     for message in x_fine:
-        start(message, early)
+        start(message, gx > 0)
 
     coarse_lane = lax.broadcasted_iota(jnp.int32, (128, FCOLS), 0)
     fine_col = lax.broadcasted_iota(jnp.int32, (128, FCOLS), 1)
@@ -305,17 +319,16 @@
             base[v, l] = total
         return carry
 
-    lax.fori_loop(0, 5, fine_step, 0)
-    pl.when(late)(lambda: pl.semaphore_wait(answer, answered))
-    signal(known, partner, late)
-    pl.when(late)(lambda: pl.semaphore_wait(known, 1))
-    for s in range(2):
-        signal(ready, near[s], jnp.logical_and(going[s], late))
+    lax.fori_loop(0, 3, fine_step, 0)
+    send_corners(between)
+    for message in y_fine:
+        start(message, between)
+    lax.fori_loop(3, 10, fine_step, 0)
+    hear(lowest)
     for message in x_row + x_fine:
-        start(message, late)
-    lax.fori_loop(5, 10, fine_step, 0)
-    send_corners(late)
+        start(message, lowest)
     lax.fori_loop(10, LEVS, fine_step, 0)
+    send_corners(lowest)
 
     relays = []
     for s in range(2):
@@ -431,32 +444,41 @@
     def inside(e):
         return jnp.where(within(e), 1.0, 0.0).astype(F32)
 
+    def kept(value, e):
+        return value if 5 <= e < 11 else value * inside(e)
+
     def fill(f, e, body, u, at, width):
         left = pltpu.roll(xm[0, u], (128 - width - at) % 128, 1)
         right = pltpu.roll(xm[1, u], (COLS - at) % 128, 1)
         value = jnp.where(lane < COLS, body, jnp.where(lane >= 112, left, right))
         if not 5 <= e < 11:
             value = jnp.where(within(e), value, 0.0)
+        if f in (3, 4):
+            value = 0.125 * value
         q[f, e] = value
 
-    for f in range(FIELDS):
-        for j in range(ROWS):
-            if f < 5:
-                body = cwo[f, j]
-            else:
-                body = jnp.concatenate([imo[f - 5, j], jnp.zeros((24, 32), F32)], axis=1)
-            fill(f, 5 + j, body, j, *SEG_ROW[f])
+    places = {}
     for s in range(2):
         for i, (f, k) in enumerate(ITEMS):
-            g, m = i // 4, i % 4
-            if m < 3:
-                body = yp[s, 3 * g + m]
-            else:
-                pieces = [pltpu.roll(yp[s, 3 * g + n], 32 + 32 * n, 1) for n in range(3)]
-                body = jnp.where(
-                    lane < 32, pieces[0], jnp.where(lane < 64, pieces[1], pieces[2])
-                )
-            fill(f, 5 - k if s == 0 else 10 + k, body, 6 + s, *SEG_CORNER[f, k])
+            places[f, 5 - k if s == 0 else 10 + k] = (s, i // 4, i % 4, k)
+
+    def fill_row(fields, e):
+        for f in fields:
+            if 5 <= e < 11:
+                if f < 5:
+                    body = cwo[f, e - 5]
+                else:
+                    side = jnp.zeros((24, 128 - COLS), F32)
+                    body = jnp.concatenate([imo[f - 5, e - 5], side], axis=1)
+                fill(f, e, body, e - 5, *SEG_ROW[f])
+            elif (f, e) in places:
+                s, g, m, k = places[f, e]
+                if m < 3:
+                    body = yp[s, 3 * g + m]
+                else:
+                    third = [pltpu.roll(yp[s, 3 * g + n], 32 + 32 * n, 1) for n in range(3)]
+                    body = jnp.where(lane < 32, third[0], jnp.where(lane < 64, third[1], third[2]))
+                fill(f, e, body, 6 + s, *SEG_CORNER[f, k])
 
     def east(x):
         return pltpu.roll(x, 127, 1)
@@ -466,14 +488,6 @@
 
     def vertical(x):
         return pltpu.roll(x, 23, 0) * above + pltpu.roll(x, 1, 0) * below
-
-    def forward(ref, base, v, e, wu, wv):
-        k = MIX[v]
-        x = ref[base + v, e]
-        total = (1.0 - 4.0 * k - 0.2) * x + vertical(x)
-        total += (k - wu) * east(x) + (k + wu) * west(x)
-        total += (k - wv) * ref[base + v, e + 1] + (k + wv) * ref[base + v, e - 1]
-        return x, total
 
     def adjoint(ref, v, e, wu, wn, ws):
         k = MIX[v]
@@ -483,77 +497,86 @@
         total += (k + wn) * ref[v, e + 1] + (k - ws) * ref[v, e - 1]
         return x, total
 
-    def slope(x):
-        t = jnp.tanh(x)
-        return t, 0.3 - 0.3 * t * t
-
     def winds(e):
-        return 0.125 * q[3, e], 0.125 * q[4, e]
+        return q[3, e], q[4, e]
+
+    def weights(v, wu, wv):
+        k = MIX[v]
+        return k - wu, k + wu, k - wv, k + wv
+
+    def centre(v, x):
+        return (0.8 - 4.0 * MIX[v]) * x + vertical(x)
+
+    def forward(ref, base, v, e, coefficients):
+        to_east, to_west, to_north, to_south = coefficients
+        x = ref[base + v, e]
+        total = centre(v, x) + to_east * east(x) + to_west * west(x)
+        total += to_north * ref[base + v, e + 1] + to_south * ref[base + v, e - 1]
+        return x, total
 
     def stage_one(e, carry):
         wu, wv = winds(e)
-        keep = inside(e)
         for v in range(VARS):
-            _, s = slope(q[v, e])
-            sc[v, e] = s
-            x, total = forward(q, 5, v, e, wu, wv)
-            d1[v, e] = (total - s * x) * keep
+            coefficients = weights(v, wu, wv)
+            t = jnp.tanh(q[v, e])
+            s = 0.3 - 0.3 * t * t
+            if 4 <= e < 12:
+                sc[v, e] = s
+            x, total = forward(q, 5, v, e, coefficients)
+            d1[v, e] = kept(total - s * x, e)
+            if 2 <= e < 14:
+                _, total = forward(q, 0, v, e, coefficients)
+                t = jnp.tanh(total - 0.3 * t)
+                st[v, e] = 0.3 - 0.3 * t * t
         return carry
 
-    for e in range(1, 15):
-        stage_one(e, 0)
-
-    def stage_path(e, carry):
+
+    def stage_two(e, carry):
         wu, wv = winds(e)
         for v in range(VARS):
-            x, total = forward(q, 0, v, e, wu, wv)
-            _, s = slope(total - 0.3 * jnp.tanh(x))
-            st[v, e] = s
+            x, total = forward(d1, 0, v, e, weights(v, wu, wv))
+            res[v, e] = kept(total - st[v, e] * x - q[8 + v, e], e)
         return carry
 
-    for e in range(2, 14):
-        stage_path(e, 0)
-
-    def stage_two(e, carry):
-        wu, wv = winds(e)
-        keep = inside(e)
-        for v in range(VARS):
-            x, total = forward(d1, 0, v, e, wu, wv)
-            res[v, e] = (total - st[v, e] * x - q[8 + v, e]) * keep
-        return carry
-
-    for e in range(2, 14):
-        stage_two(e, 0)
 
     def stage_three(e, carry):
         wu, _ = winds(e)
-        keep = inside(e)
-        wn, ws = 0.125 * q[4, e + 1], 0.125 * q[4, e - 1]
+        wn, ws = q[4, e + 1], q[4, e - 1]
         for v in range(VARS):
             x, total = adjoint(res, v, e, wu, wn, ws)
-            a1[v, e] = (total - st[v, e] * x) * keep
+            a1[v, e] = kept(total - st[v, e] * x, e)
         return carry
 
-    for e in range(3, 13):
-        stage_three(e, 0)
 
     def stage_four(e, carry):
         wu, _ = winds(e)
-        keep = inside(e)
-        wn, ws = 0.125 * q[4, e + 1], 0.125 * q[4, e - 1]
+        wn, ws = q[4, e + 1], q[4, e - 1]
         for v in range(VARS):
             x, total = adjoint(a1, v, e, wu, wn, ws)
             start = q[5 + v, e]
             slant = start + total - sc[v, e] * x
-            up[v, e - 4] = (start - 0.5 * slant) * keep
-            q[v, e] = slant
+            up[v, e - 4] = kept(start - 0.5 * slant, e)
+            if 5 <= e < 11:
+                grad[v, e - 5] = slant[0:16, 0:COLS]
         return carry
 
-    for e in range(4, 12):
-        stage_four(e, 0)
-    for v in range(VARS):
-        for j in range(ROWS):
-            grad[v, j] = q[v, 5 + j, 0:16, 0:COLS]
+    for front in range(16 + 4):
+        if front < 16:
+            fill_row(range(8), front)
+        e = front - 1
+        if 1 <= e < 15:
+            stage_one(e, 0)
+        e = front - 2
+        if 2 <= e < 14:
+            fill_row(range(8, 11), e)
+            stage_two(e, 0)
+        e = front - 3
+        if 3 <= e < 13:
+            stage_three(e, 0)
+        e = front - 4
+        if 4 <= e < 12:
+            stage_four(e, 0)
+
     grad_copy = pltpu.make_async_copy(grad, gradient, out_sem.at[6])
     grad_copy.start()
 
@@ -584,12 +607,16 @@
             vr[1, at, :] = mixed[0:16]
             vr[2, at, :] = 0.125 * (south - north)[0:16]
             south, here = here, north
-        for l in range(LEVS):
-            at = pl.ds(24 * l, 24)
-            by_level = pl.ds(l, 24, stride=24)
-            lv[at, 256:384], lv[at, 384:512] = two_parts(vr[0, by_level, :])
-            lv[at, 0:128], lv[at, 128:256] = two_parts(vr[1, by_level, :])
-            ly[at, 0:128], ly[at, 128:256] = two_parts(vr[2, by_level, :])
+        for l in range(0, LEVS, 2):
+            at = pl.ds(24 * l, 48)
+
+            def pair(i):
+                one, two = vr[i, pl.ds(l, 24, stride=24), :], vr[i, pl.ds(l + 1, 24, stride=24), :]
+                return two_parts(jnp.concatenate([one, two], axis=0))
+
+            lv[at, 256:384], lv[at, 384:512] = pair(0)
+            lv[at, 0:128], lv[at, 128:256] = pair(1)
+            ly[at, 0:128], ly[at, 128:256] = pair(2)
         for c in range(2):
             at = slice(192 * c, 192 * c + 192)
             levels = slice(8 * c, 8 * c + 8)
@@ -598,10 +625,11 @@
             def dot(x, t):
                 return jnp.dot(x, t, preferred_element_type=F32).reshape(shape)
 
-            step = dot(lv[at, 256:512], table_a[:, 0:FCOLS])
+            both = jnp.dot(lv[at, 256:512], table_a[...], preferred_element_type=F32)
+            step = both[:, 0:FCOLS].reshape(shape)
             total = base[v, levels] - 0.3 * jnp.tanh(fs[v, levels] + step)
+            total += wf[0, levels] * both[:, FCOLS:].reshape(shape)
             total += k * dot(lv[at, :], table_b[...])
-            total += wf[0, levels] * dot(lv[at, 256:512], table_a[:, FCOLS:])
             total += wf[1, levels] * dot(ly[at, :], table_a[:, 0:FCOLS])
             out[v, levels] = total
             copy = pltpu.make_async_copy(

time: 22.2 us -> 21.5 us (0.968)
  Pallas kernels: 21.5 us -> 20.6 us
    pallas_call x1, Pallas kernels: 15.8 us -> 15 us  [exchange(): pl.pallas_call(exchange_kernel, out_shape=(pltpu.VMEM((VARS, LEVS, FROWS,...]
where the time goes in v5:
time: 21.5 us; the launch traced here: 21.2 us
  Pallas kernels  20.6 us (96%)
  between operations  0.64 us (3%)
    pallas_call x1, Pallas kernels, exchange(): pl.pallas_call(exchange_kernel, out_shape=(pltpu.VMEM((VARS, LEVS, FROWS,...  15 us
    pallas_call x1, Pallas kernels, solve(): pl.pallas_call(solve_kernel, out_shape=(jax.ShapeDtypeStruct((VARS, LEVS,...  5.58 us

profile of v5, /device:TPU:25, one launch (start us, length us, event | category | flops | bytes accessed | tf_op | source)
XLA Modules:
  0.0 21.2 jit_solution(7524067580635916469)
XLA Ops:
  0.6 15.0 %exchange.1 = (f32[3,16,24,384]{3,2,1,0:T(8,128)S(1)}, f32[2,16,24,384]{3,2,1,0:T(8,128)S(1)}, f32[3,16,24,384]{3,2,1,0:T(8,128)S(1)}, f32[2,33,24,128]{3,2,1,0:...) custom-call(f32[3,16,24,384]{3,2,1,0:T(8,128)} %fine.1, ...), custom_call_target="tpu_custom_call" | custom-call | tf_op jit(solution)/shard_map/exchange/pallas_call | solution.py:386
  15.7 5.6 %solve.1 = (f32[3,16,24,384]{3,2,1,0:T(8,128)}, f32[3,6,16,96]{3,2,1,0:T(8,128)}) custom-call(f32[3,16,24,384]{3,2,1,0:T(8,128)S(1)} %get-tuple-element.13.fs, f32[2,16,24,384]{3,2,1,0:T(8,128)S(1)} %get-tuple-element.14.wf, f32[3,16,24,384]{3,2,1,0:T(8,128)S(1)} %get-tuple-element.15.base, f32[2,33,24,128]{3,2,1,0:T(8,128)S(1)} %get-tuple-element.16.yp, ...), custom_call_target="tpu_custom_call" | custom-call | tf_op jit(solution)/shard_map/solve/pallas_call | solution.py:647

commit v6 on v5

--- a/solution.py
+++ b/solution.py
@@ -319,11 +319,10 @@
             base[v, l] = total
         return carry
 
-    lax.fori_loop(0, 3, fine_step, 0)
     send_corners(between)
     for message in y_fine:
         start(message, between)
-    lax.fori_loop(3, 10, fine_step, 0)
+    lax.fori_loop(0, 10, fine_step, 0)
     hear(lowest)
     for message in x_row + x_fine:
         start(message, lowest)
@@ -353,7 +352,7 @@
                 base[v, l, rows, 256:384] += jnp.where(lane8 == 127, (k - wu1) * right, 0.0)
         return carry
 
-    lax.fori_loop(0, LEVS, fine_columns, 0)
+    lax.fori_loop(0, LEVS, fine_columns, 0, unroll=2)
     for v in range(VARS):
         base[v, edge] += 0.1 * fl[v]
 
@@ -372,7 +371,7 @@
             base[v, l, 16:24] += (k - 0.125 * wf[1, l, 16:24]) * north
         return carry
 
-    lax.fori_loop(0, LEVS, fine_rows, 0)
+    lax.fori_loop(0, LEVS, fine_rows, 0, unroll=4)
     for message in own + relays + x_row + corner:
         arrive(message)
     for copy, goes in started:

time: 21.5 us -> 21.4 us (level)
  no operation moved by 1% of the time
where the time goes in v6:
time: 21.4 us; the launch traced here: 21.2 us
  Pallas kernels  20.6 us (96%)
  between operations  0.64 us (3%)
    pallas_call x1, Pallas kernels, exchange(): pl.pallas_call(exchange_kernel, out_shape=(pltpu.VMEM((VARS, LEVS, FROWS,...  15 us
    pallas_call x1, Pallas kernels, solve(): pl.pallas_call(solve_kernel, out_shape=(jax.ShapeDtypeStruct((VARS, LEVS,...  5.58 us

profile of v6, /device:TPU:25, one launch (start us, length us, event | category | flops | bytes accessed | tf_op | source)
XLA Modules:
  0.0 21.2 jit_solution(6718571591367397909)
XLA Ops:
  0.6 15.0 %exchange.1 = (f32[3,16,24,384]{3,2,1,0:T(8,128)S(1)}, f32[2,16,24,384]{3,2,1,0:T(8,128)S(1)}, f32[3,16,24,384]{3,2,1,0:T(8,128)S(1)}, f32[2,33,24,128]{3,2,1,0:...) custom-call(f32[3,16,24,384]{3,2,1,0:T(8,128)} %fine.1, ...), custom_call_target="tpu_custom_call" | custom-call | tf_op jit(solution)/shard_map/exchange/pallas_call | solution.py:385
  15.7 5.6 %solve.1 = (f32[3,16,24,384]{3,2,1,0:T(8,128)}, f32[3,6,16,96]{3,2,1,0:T(8,128)}) custom-call(f32[3,16,24,384]{3,2,1,0:T(8,128)S(1)} %get-tuple-element.13.fs, f32[2,16,24,384]{3,2,1,0:T(8,128)S(1)} %get-tuple-element.14.wf, f32[3,16,24,384]{3,2,1,0:T(8,128)S(1)} %get-tuple-element.15.base, f32[2,33,24,128]{3,2,1,0:T(8,128)S(1)} %get-tuple-element.16.yp, ...), custom_call_target="tpu_custom_call" | custom-call | tf_op jit(solution)/shard_map/solve/pallas_call | solution.py:646
